TPU v7x, 128 devices: a whole 4x4x4 slice. The times are simulated.
128 devices in a mesh: seq: 8 (over z, core), tp: 16 (over y, x).
Axes of the slice: x: 4, y: 4, z: 4, core: 2. Of those that a mesh axis runs over, the one named last changes fastest.
Arguments:
- inputs: bfloat16 [8192, 4096], P('seq'), may hold values from -6 to 6
- cotangent: bfloat16 [8192, 4096], P('seq'), may hold values from -6 to 6
- w_in: bfloat16 [4096, 5120], P(None, 'tp'), may hold values from -0.125 to 0.125
- conv_w: float32 [3, 5120], P(None, 'tp'), may hold values from -3.5 to 3.5
- norm_gain: float32 [4096], P('tp'), may hold values from 0.25 to 1.75
- w_out: bfloat16 [4096, 4096], P('tp'), may hold values from -0.125 to 0.125
- keep_flags: int32 [32], P('tp'), may hold values 0 or 1
Outputs:
- layer_out: bfloat16 [8192, 4096], P('seq', 'tp')
- input_grad: bfloat16 [8192, 4096], P('seq', 'tp')
All inputs are finite; a program needn't handle non-finite values. No bound on the sum of `keep_flags` on one device may be relied on, other than what follows from the above.
Results may differ from a plain program's by a relative error of at most 0.0071.
Values may be sent and summed in bfloat16 or wider, within the bound.
A program may use at most 192 MiB of HBM per device.

v0:
```python
from functools import partial

import jax
import jax.numpy as jnp
import numpy as np
from jax import lax
from jax.experimental import pallas as pl
from jax.experimental.pallas import tpu as pltpu
from jax.sharding import PartitionSpec as P

FEAT = 16
DV = 128
LANES = 384
EXP = 256
HEADS = 2
epsilon = 1e-06

CH = 256
NCH = 4
MESH = pl.DeviceIdType.MESH
NT = (((1,), (1,)), ((), ()))
NN = (((1,), (0,)), ((), ()))
TN = (((0,), (0,)), ((), ()))
f32 = jnp.float32
bf16 = jnp.bfloat16


def neighbour(along, step):
    place = lax.axis_index("tp")
    column, row = lax.rem(place, 4), lax.div(place, 4)
    if along == "x":
        return row * 4 + lax.rem(column + step, 4)
    return lax.rem(row + step, 4) * 4 + column


def block_at(a_along, a_step, r_along, r_step):
    place = lax.axis_index("tp")
    column, row = lax.rem(place, 4), lax.div(place, 4)
    x_step = a_step if a_along == "x" else r_step
    y_step = a_step if a_along == "y" else r_step
    return lax.rem(row + y_step, 4) * 4 + lax.rem(column + x_step, 4)


def to_device(src, dst, send_sem, recv_sem, place):
    return pltpu.make_async_remote_copy(
        src_ref=src,
        dst_ref=dst,
        send_sem=send_sem,
        recv_sem=recv_sem,
        device_id={"tp": place},
        device_id_type=MESH,
    )


def rows_of(c):
    return pl.ds(pl.multiple_of(c * CH, CH), CH)


def way(c):
    return jnp.where(c < NCH // 2, 1, 3)


class Ring:
    def __init__(self, a, r, held, weight, own, dims, part, landed, relay, keep, res, out, sems):
        self.a, self.r = a, r
        self.held, self.weight, self.own, self.dims = held, weight, own, dims
        self.part, self.landed, self.relay = part, landed, relay
        self.keep, self.res, self.out = keep, res, out
        (self.gs, self.gr, self.ts, self.tr, self.ps, self.pr, self.ws, self.wr, self.wo) = sems

    def weight_copies(self, w_block):
        copies = []
        for d in range(1, 4):
            for k in range(4):
                src = w_block(block_at(self.a, d, self.r, k))
                copies.append(
                    to_device(
                        src,
                        self.weight.at[k, d],
                        self.ws.at[d - 1, k],
                        self.wr.at[d - 1, k],
                        neighbour(self.a, d),
                    )
                )
        return copies

    def own_copies(self, w_block):
        return [
            pltpu.make_async_copy(
                w_block(block_at(self.a, 0, self.r, k)), self.weight.at[k, 0], self.wo.at[k]
            )
            for k in range(4)
        ]

    def direct(self, c, d):
        return to_device(
            self.held.at[0, rows_of(c)],
            self.held.at[d, rows_of(c)],
            self.gs.at[d - 1, c],
            self.gr.at[d - 1, c],
            neighbour(self.a, d),
        )

    def passed_on(self, c):
        return to_device(
            self.held.at[way(c), rows_of(c)],
            self.held.at[2, rows_of(c)],
            self.gs.at[1, c],
            self.gr.at[1, c],
            neighbour(self.a, way(c)),
        )

    def send_own(self, c):
        self.direct(c, 1).start()
        self.direct(c, 3).start()

    def forward(self, c):
        self.direct(c, 1).wait_recv()
        self.direct(c, 3).wait_recv()
        self.passed_on(c).start()

    def tie(self, c):
        return to_device(
            self.part.at[2, rows_of(c)],
            self.relay.at[rows_of(c)],
            self.ts.at[c],
            self.tr.at[c],
            neighbour(self.r, way(c)),
        )

    def side(self, c, d):
        return to_device(
            self.part.at[d, rows_of(c)],
            self.landed.at[d // 2, rows_of(c)],
            self.ps.at[d // 2, c],
            self.pr.at[d // 2, c],
            neighbour(self.r, d),
        )

    def product(self, c, k):
        total = None
        for o in range(4):
            term = lax.dot_general(
                self.held[o, rows_of(c)], self.weight[k, o], self.dims, preferred_element_type=f32
            )
            total = term if total is None else total + term
        return total

    def multiply(self, c):
        self.passed_on(c).wait_recv()
        near, far = way(c), 4 - way(c)
        self.part[2, rows_of(c)] = self.product(c, 2).astype(bf16)
        self.tie(c).start()
        self.part[far, rows_of(c)] = self.product(c, far).astype(bf16)
        self.side(c, far).start()
        self.keep[1, rows_of(c)] = self.product(c, near)
        self.keep[0, rows_of(c)] = self.product(c, 0) + self.res[rows_of(c)].astype(f32)

    def relayed(self, c):
        self.tie(c).wait_recv()
        near = way(c)
        total = self.keep[1, rows_of(c)] + self.relay[rows_of(c)].astype(f32)
        self.part[near, rows_of(c)] = total.astype(bf16)
        self.side(c, near).start()

    def finish(self, c):
        self.side(c, 1).wait_recv()
        self.side(c, 3).wait_recv()
        total = self.keep[0, rows_of(c)] + (
            self.landed[0, rows_of(c)].astype(f32) + self.landed[1, rows_of(c)].astype(f32)
        )
        self.out[rows_of(c)] = total.astype(bf16)

    def drain(self, c):
        self.direct(c, 1).wait_send()
        self.direct(c, 3).wait_send()
        self.passed_on(c).wait_send()
        self.tie(c).wait_send()
        self.side(c, 1).wait_send()
        self.side(c, 3).wait_send()


def ring_semaphores():
    dma = pltpu.SemaphoreType.DMA
    return [
        dma((3, NCH)),
        dma((3, NCH)),
        dma((NCH,)),
        dma((NCH,)),
        dma((2, NCH)),
        dma((2, NCH)),
        dma((3, 4)),
        dma((3, 4)),
        dma((4,)),
    ]


def ring_buffers(rows, width, weight_shape):
    return [
        pltpu.VMEM((4, rows, width), bf16),
        pltpu.VMEM((4, 4) + weight_shape, bf16),
        pltpu.VMEM((4, rows, 256), bf16),
        pltpu.VMEM((2, rows, 256), bf16),
        pltpu.VMEM((rows, 256), bf16),
        pltpu.VMEM((2, rows, 256), f32),
        pltpu.VMEM((rows, 256), bf16),
    ]


def selectors():
    first = np.zeros((4, 128, EXP), np.float32)
    second = np.zeros((4, 128, EXP), np.float32)
    rows = np.zeros((8, EXP), np.float32)
    rows[0, 0] = rows[1, 0] = rows[2, 0] = 1.0
    for group in range(4):
        base = group * FEAT
        for i in range(FEAT):
            first[group, base + i, 1 + i] = 1.0
            rows[1, 1 + i] = 1.0
            rows[2, 1 + i] = 0.25
        e = 1 + FEAT
        for i in range(FEAT):
            for j in range(i, FEAT):
                first[group, base + i, e] = 1.0
                second[group, base + j, e] = 1.0
                rows[2, e] = 1 / 32 if i == j else 1 / 16
                e += 1
    moves = np.zeros((4, 128, 128), np.float32)
    for h in range(HEADS):
        for i in range(FEAT):
            q, k = 2 * h * FEAT + i, (2 * h + 1) * FEAT + i
            moves[2 * h, q, k] = 1.0
            moves[2 * h + 1, k, q] = 1.0
    return first, second, rows, moves


def dot(a, b, dims=NN):
    return lax.dot_general(a, b, dims, preferred_element_type=f32)


def one_if(condition):
    return jnp.where(condition, 1.0, 0.0).astype(f32)


def to_seq(src, dst, send_sem, recv_sem, place):
    return pltpu.make_async_remote_copy(
        src_ref=src,
        dst_ref=dst,
        send_sem=send_sem,
        recv_sem=recv_sem,
        device_id={"seq": place},
        device_id_type=MESH,
    )


class Carry:
    def __init__(self, earlier, local, state, bufs, sems):
        self.earlier, self.local, self.state = earlier, local, state
        self.sa, self.ra, self.sb, self.rb, self.sc, self.rc = bufs
        self.pair_sems, self.zs, self.zr = sems
        place = lax.axis_index("seq")
        self.core, self.z = lax.rem(place, 2), lax.div(place, 2)
        self.partner = self.z * 2 + (1 - self.core)

    def swap(self):
        return to_seq(self.sa, self.ra, self.pair_sems.at[0], self.pair_sems.at[1], self.partner)

    def give(self):
        return to_seq(self.sc, self.rc, self.pair_sems.at[2], self.pair_sems.at[3], self.partner)

    def along(self, step):
        there = lax.rem(self.z + step, 4) * 2 + self.core
        return to_seq(
            self.sb, self.rb.at[step - 1], self.zs.at[step - 1], self.zr.at[step - 1], there
        )

    def start(self):
        self.sa[...] = self.local[1 - self.core].astype(bf16)
        self.swap().start()

    def middle(self):
        self.swap().wait_recv()
        self.sb[...] = (self.local[self.core] + self.ra[...].astype(f32)).astype(bf16)
        for step in (1, 2, 3):
            self.along(step).start()

    def late(self):
        total = jnp.zeros(self.sb.shape, f32)
        for step in (1, 2, 3):
            self.along(step).wait_recv()
            counts = one_if(self.z >= step if self.earlier else self.z < step)
            total = total + self.rb[step - 1].astype(f32) * counts
        takes = self.core if self.earlier else 1 - self.core
        self.sc[...] = (total + self.local[self.core] * one_if(takes == 0)).astype(bf16)
        self.give().start()
        self.state[self.core] = total + self.ra[...].astype(f32) * one_if(takes == 1)

    def end(self):
        self.give().wait_recv()
        self.state[1 - self.core] = self.rc[...].astype(f32)

    def drain(self):
        self.swap().wait_send()
        self.give().wait_send()
        for step in (1, 2, 3):
            self.along(step).wait_send()


def layer_kernel(
    inputs, cotangent, w_t, w_out, taps, gains, first, second, rows, moves,
    layer_out, input_grad, *scratch,
):
    take = list(scratch)

    def pop(n):
        got = take[:n]
        del take[:n]
        return got

    fwd_bufs, bwd_bufs = pop(7), pop(7)
    fwd_sems, bwd_sems = pop(9), pop(9)
    early_bufs, late_bufs = pop(6), pop(6)
    early_sems, late_sems = pop(3), pop(3)
    (xin, cot, weights_t, weights_o) = pop(4)
    (pp, cv, mix, gh, dn, phi_q, phi_k, states, grads, scaled, dconv) = pop(11)
    (state_in, state_out, local_in, local_out, halo_in, halo_out) = pop(6)
    (x_sem, c_sem, w_sem, o_sem, r_sem, h_sem) = pop(6)

    tp, place = lax.axis_index("tp"), lax.axis_index("seq")

    def ring(a, r, bufs, sems, out):
        held, weight, part, landed, relay, keep, res = bufs
        return Ring(a, r, held, weight, None, NN, part, landed, relay, keep, res, out, sems)

    fwd = ring("x", "y", fwd_bufs, fwd_sems, layer_out)
    bwd = ring("y", "x", bwd_bufs, bwd_sems, input_grad)
    early = Carry(True, local_in, state_in, early_bufs, early_sems)
    later = Carry(False, local_out, state_out, late_bufs, late_sems)
    heads, d_proj = fwd.held.at[0], bwd.held.at[0]

    def columns(t):
        return pl.ds(pl.multiple_of(t * 256, 256), 256)

    def out_block(t):
        return w_out.at[:, columns(t)]

    def in_block(t):
        return weights_t.at[pl.ds(0, 320), columns(t)]

    pieces = ((32, 128, 0), (192, 128, 128), (0, 32, 256), (160, 32, 288))
    w_loads = [
        pltpu.make_async_copy(
            w_t.at[pl.ds(src, size)], weights_t.at[pl.ds(dst, size)], w_sem.at[n]
        )
        for n, (src, size, dst) in enumerate(pieces)
    ]
    for copy in w_loads:
        copy.start()

    def x_load(c):
        return pltpu.make_async_copy(inputs.at[rows_of(c)], xin.at[rows_of(c)], x_sem.at[c])

    def c_load(c):
        return pltpu.make_async_copy(cotangent.at[rows_of(c)], cot.at[rows_of(c)], c_sem.at[c])

    for c in (3, 0, 1, 2):
        x_load(c).start()
    o_load = pltpu.make_async_copy(w_out, weights_o, o_sem.at[0])
    o_load.start()
    for c in range(NCH):
        c_load(c).start()
    res_loads = [
        pltpu.make_async_copy(inputs.at[:, columns(tp)], fwd.res, r_sem.at[0]),
        pltpu.make_async_copy(cotangent.at[:, columns(tp)], bwd.res, r_sem.at[1]),
    ]
    fwd_own = fwd.own_copies(out_block)
    for copy in res_loads + fwd_own:
        copy.start()

    barrier = pltpu.get_barrier_semaphore()
    for along in ("x", "y"):
        for d in (1, 2, 3):
            pl.semaphore_signal(
                barrier, inc=1, device_id={"tp": neighbour(along, d)}, device_id_type=MESH
            )
    for d in (1, 2, 4, 6, 7):
        pl.semaphore_signal(
            barrier, inc=1, device_id={"seq": lax.rem(place + d, 8)}, device_id_type=MESH
        )
    weights_t[pl.ds(320, 64)] = jnp.zeros((64, weights_t.shape[1]), bf16)
    pl.semaphore_wait(barrier, 11)
    fwd_weights = fwd.weight_copies(out_block)
    for copy in fwd_weights:
        copy.start()
    for copy in w_loads:
        copy.wait()
    bwd_own = bwd.own_copies(in_block)
    bwd_weights = bwd.weight_copies(in_block)
    for copy in bwd_weights + bwd_own:
        copy.start()

    ahead = to_seq(
        pp.at[pl.ds(NCH * CH, 8)], halo_in, h_sem.at[0], h_sem.at[1], lax.rem(place + 1, 8)
    )
    behind = to_seq(
        dconv.at[pl.ds(0, 8)], halo_out, h_sem.at[2], h_sem.at[3], lax.rem(place + 7, 8)
    )

    @pl.loop(0, NCH)
    def _(i):
        c = lax.rem(i + NCH - 1, NCH)
        x_load(c).wait()
        projected = dot(xin[rows_of(c)], weights_t[...], NT).astype(bf16).astype(f32)
        pp[pl.ds(pl.multiple_of(c * CH + 8, 8), CH)] = projected

        @pl.when(i == 0)
        def _():
            ahead.start()

    ahead.wait()
    pp[pl.ds(0, 8)] = halo_in[...] * one_if(place > 0)

    t0, t1, t2 = taps[0:1], taps[1:2], taps[2:3]
    bias_a, bias_b, scale = rows[0:1], rows[1:2], rows[2:3]

    def factors(qk, group):
        return dot(qk, first[group]) + bias_a, dot(qk, second[group]) + bias_b

    def lanes(h):
        return slice(h * DV, (h + 1) * DV)

    def qk_of(c):
        return cv[rows_of(c), 2 * DV : LANES]

    local_in[...] = jnp.zeros(local_in.shape, f32)

    @pl.loop(0, NCH)
    def _(c):
        window = pp[pl.ds(pl.multiple_of(c * CH, CH), CH + 8)]
        mixed = t0 * window[8:] + (
            t1 * pltpu.roll(window, 1, 0)[8:] + t2 * pltpu.roll(window, 2, 0)[8:]
        )
        cv[rows_of(c)] = mixed.astype(bf16)
        qk = qk_of(c)
        for h in range(HEADS):
            a, b = factors(qk, 2 * h + 1)
            features = (a * b).astype(bf16)
            phi_k[h, rows_of(c)] = features
            local = dot(cv[rows_of(c), lanes(h)], features, TN)
            states[c, h] = local
            local_in[h] = local_in[h] + local

    early.start()

    causal = lax.broadcasted_iota(jnp.int32, (CH, CH), 0) >= lax.broadcasted_iota(
        jnp.int32, (CH, CH), 1
    )

    @pl.loop(0, NCH)
    def _(c):
        qk = qk_of(c)
        for h in range(HEADS):
            logits = dot(dot(qk, moves[2 * h]).astype(bf16), qk, NT) * 0.25
            weight = jnp.where(causal, 1.0 + logits + 0.5 * logits * logits, 0.0)
            mix[rows_of(c), lanes(h)] = dot(weight.astype(bf16), cv[rows_of(c), lanes(h)])

        @pl.when(c == 1)
        def _():
            early.middle()

    o_load.wait()
    gain = gains[0:1]

    @pl.loop(0, NCH)
    def _(c):
        c_load(c).wait()
        gh[rows_of(c)] = dot(cot[rows_of(c)], weights_o[...], NT) * gain

    early.late()

    @pl.loop(0, NCH)
    def _(c):
        qk = qk_of(c)
        for h in range(HEADS):
            a, b = factors(qk, 2 * h)
            phi_q[h, rows_of(c)] = (a * b).astype(bf16)

    early.end()
    local_out[...] = jnp.zeros(local_out.shape, f32)

    @pl.loop(0, NCH)
    def _(c):
        for h in range(HEADS):
            entering = state_in[h]
            state_in[h] = entering + states[c, h]
            scaled[c, h] = (entering * scale).astype(bf16)
            numerator = mix[rows_of(c), lanes(h)] + dot(phi_q[h, rows_of(c)], scaled[c, h], NT)
            inverse = 1.0 / jnp.sqrt(jnp.mean(numerator * numerator, -1, keepdims=True) + epsilon)
            normed = numerator * inverse
            heads[rows_of(c), lanes(h)] = (normed * gain[:, lanes(h)]).astype(bf16)
            grad = gh[rows_of(c), lanes(h)]
            d_numer = (grad - normed * jnp.mean(grad * normed, -1, keepdims=True)) * inverse
            rounded = d_numer.astype(bf16)
            dn[rows_of(c), lanes(h)] = rounded
            local = dot(rounded, phi_q[h, rows_of(c)], TN)
            grads[c, h] = local
            local_out[h] = local_out[h] + local
        fwd.send_own(c)

    later.start()

    @pl.loop(0, NCH)
    def _(c):
        qk = qk_of(c)
        d_qk = jnp.zeros((CH, 128), f32)
        for h in range(HEADS):
            moved = dot(qk, moves[2 * h]).astype(bf16)
            logits = dot(moved, qk, NT) * 0.25
            weight = jnp.where(causal, 1.0 + logits + 0.5 * logits * logits, 0.0)
            rounded = dn[rows_of(c), lanes(h)]
            dconv[rows_of(c), lanes(h)] = dot(weight.astype(bf16), rounded, TN)
            d_weight = dot(rounded, cv[rows_of(c), lanes(h)], NT)
            d_logits = jnp.where(causal, d_weight * (1.0 + logits), 0.0) * 0.25
            d_logits = d_logits.astype(bf16)
            d_qk = d_qk + dot(d_logits, dot(qk, moves[2 * h + 1]).astype(bf16))
            d_qk = d_qk + dot(d_logits, moved, TN)
            a, b = factors(qk, 2 * h)
            d_phi = dot(rounded, scaled[c, h])
            d_qk = d_qk + dot((d_phi * b).astype(bf16), first[2 * h], NT)
            d_qk = d_qk + dot((d_phi * a).astype(bf16), second[2 * h], NT)
        dconv[rows_of(c), 2 * DV : LANES] = d_qk

        @pl.when(c == 1)
        def _():
            later.middle()

        @pl.when(c == 3)
        def _():
            later.late()

        fwd.forward(c)

    for copy in fwd_weights + fwd_own + res_loads:
        copy.wait()
    later.end()
    state_out[...] = state_out[...] + local_out[...]

    def project_back(c):
        window = dconv[pl.ds(pl.multiple_of(c * CH, CH), CH + 8)]
        mixed = t0 * window[:CH] + (
            t1 * pltpu.roll(window, CH + 7, 0)[:CH] + t2 * pltpu.roll(window, CH + 6, 0)[:CH]
        )
        d_proj[rows_of(c)] = mixed[:, :320].astype(bf16)
        bwd.send_own(c)

    @pl.loop(0, NCH)
    def _(c):
        qk = qk_of(c)
        d_qk = dconv[rows_of(c), 2 * DV : LANES]
        for h in range(HEADS):
            remaining = state_out[h] - grads[c, h]
            state_out[h] = remaining
            suffix = (remaining * scale).astype(bf16)
            dconv[rows_of(c), lanes(h)] = dconv[rows_of(c), lanes(h)] + dot(
                phi_k[h, rows_of(c)], suffix, NT
            )
            a, b = factors(qk, 2 * h + 1)
            d_phi = dot(cv[rows_of(c), lanes(h)], suffix)
            d_qk = d_qk + dot((d_phi * b).astype(bf16), first[2 * h + 1], NT)
            d_qk = d_qk + dot((d_phi * a).astype(bf16), second[2 * h + 1], NT)
        dconv[rows_of(c), 2 * DV : LANES] = d_qk

        @pl.when(c == 0)
        def _():
            behind.start()

        @pl.when(c > 0)
        def _():
            project_back(c - 1)

        fwd.multiply(c)

    behind.wait()
    dconv[pl.ds(NCH * CH, 8)] = halo_out[...] * one_if(place < 7)
    project_back(NCH - 1)
    for copy in bwd_weights + bwd_own:
        copy.wait()

    @pl.loop(0, NCH + 3)
    def _(i):
        @pl.when(i < NCH)
        def _():
            bwd.forward(i)
            fwd.relayed(i)

        @pl.when((i >= 1) & (i < NCH + 1))
        def _():
            bwd.multiply(i - 1)

        @pl.when((i >= 2) & (i < NCH + 2))
        def _():
            bwd.relayed(i - 2)
            fwd.finish(i - 2)

        @pl.when(i >= 3)
        def _():
            bwd.finish(i - 3)

    @pl.loop(0, NCH)
    def _(c):
        fwd.drain(c)
        bwd.drain(c)

    early.drain()
    later.drain()


def permuted(array):
    parts = [array[..., 32:160], array[..., 192:320], array[..., 0:32], array[..., 160:192]]
    return jnp.concatenate(parts + [jnp.zeros(array.shape[:-1] + (64,), array.dtype)], -1)


def per_device(inputs, cotangent, w_in, conv_w, norm_gain, w_out, keep_flags):
    count, width = inputs.shape
    taps = jnp.pad(permuted(conv_w), ((0, 5), (0, 0)))
    gains = (norm_gain.reshape(HEADS, DV) * keep_flags.astype(f32)[:, None]).reshape(1, HEADS * DV)
    first, second, rows, moves = selectors()
    consts = [jnp.asarray(first, bf16), jnp.asarray(second, bf16), jnp.asarray(rows), jnp.asarray(moves, bf16)]
    whole, near = pl.BlockSpec(memory_space=pl.ANY), pl.BlockSpec(memory_space=pltpu.VMEM)
    result = jax.ShapeDtypeStruct((count, 256), bf16)
    dma = pltpu.SemaphoreType.DMA
    state = (DV, EXP)
    carry_bufs = [pltpu.VMEM((n,) + state if n > 1 else state, bf16) for n in (1, 1, 1, 3, 1, 1)]
    carry_sems = [dma((4,)), dma((3,)), dma((3,))]
    return pl.pallas_call(
        layer_kernel,
        out_shape=(result, result),
        in_specs=[whole] * 4 + [near] * 6,
        out_specs=(near, near),
        scratch_shapes=ring_buffers(count, 256, (256, 256))
        + ring_buffers(count, 320, (320, 256))
        + ring_semaphores()
        + ring_semaphores()
        + carry_bufs
        + carry_bufs
        + carry_sems
        + carry_sems
        + [
            pltpu.VMEM((count, width), bf16),
            pltpu.VMEM((count, width), bf16),
            pltpu.VMEM((LANES, width), bf16),
            pltpu.VMEM((256, width), bf16),
            pltpu.VMEM((count + 8, LANES), f32),
            pltpu.VMEM((count, LANES), bf16),
            pltpu.VMEM((count, 256), f32),
            pltpu.VMEM((count, 256), f32),
            pltpu.VMEM((count, 256), bf16),
            pltpu.VMEM((HEADS, count, EXP), bf16),
            pltpu.VMEM((HEADS, count, EXP), bf16),
            pltpu.VMEM((NCH, HEADS) + state, f32),
            pltpu.VMEM((NCH, HEADS) + state, f32),
            pltpu.VMEM((NCH, HEADS) + state, bf16),
            pltpu.VMEM((count + 8, LANES), f32),
            pltpu.VMEM((HEADS,) + state, f32),
            pltpu.VMEM((HEADS,) + state, f32),
            pltpu.VMEM((HEADS,) + state, f32),
            pltpu.VMEM((HEADS,) + state, f32),
            pltpu.VMEM((8, LANES), f32),
            pltpu.VMEM((8, LANES), f32),
            dma((NCH,)),
            dma((NCH,)),
            dma((4,)),
            dma((1,)),
            dma((2,)),
            dma((4,)),
        ],
        compiler_params=pltpu.CompilerParams(
            collective_id=0, has_side_effects=True, vmem_limit_bytes=62 << 20
        ),
    )(inputs, cotangent, w_in.T, w_out, taps, gains, *consts)


def solution(mesh):
    placed = (
        P("seq", None),
        P("seq", None),
        P(None, "tp"),
        P(None, "tp"),
        P("tp"),
        P("tp", None),
        P("tp"),
    )
    return jax.shard_map(
        per_device,
        mesh=mesh,
        in_specs=placed,
        out_specs=(P("seq", "tp"), P("seq", "tp")),
        check_vma=False,
    )
```

profile of v0, /device:TPU:1, one launch (start us, length us, event | category | flops | bytes accessed | tf_op | source)
XLA Modules:
  0.0 117.8 jit_solution(1209911013129469768)
XLA Ops:
  0.6 0.7 convert_element_type.5
  1.3 1.3 %bitcast_multiply_fusion = f32[256]{0:T(256)} fusion(f32[256]{0:T(256)} %param.15, f32[2]{0:T(128)S(1)} %convert_element_type.5), kind=kLoop, calls=%fused_computation | loop fusion | flops 256 | bytes 2056 | tf_op jit(solution)/shard_map/mul | solution.py:626
  2.6 0.8 fusion
  3.4 0.8 fusion.1
  4.2 0.1 concatenate.3
  4.3 0.6 pad.4.taps
  4.9 109.1 %shard_map.122 = (bf16[1024,256]{1,0:T(8,128)(2,1)}, bf16[1024,256]{1,0:T(8,128)(2,1)}) custom-call(bf16[1024,4096]{1,0:T(8,128)(2,1)} %inputs.1, bf16[1024,4096]{1,0:T(8,128)(2,1)} %cotangent.1, bf16[320,4096]{1,0:T(8,128)(2,1)} %bitcast.4, bf16[256,4096]{1,0:T(8,128)(2,1)} %w_out.1, f32[8,384]{1,0:T(8,128)} %pad.4.taps, f32[1,256]{1,0:T(1,128)} %bitcast.5, ...), custom_call_target="tpu_custom_call" | custom-call | tf_op jit(solution)/shard_map/pallas_call | solution.py:635
  114.1 1.9 %copy.15 = bf16[1024,256]{1,0:T(8,128)(2,1)} copy(bf16[1024,256]{1,0:T(8,128)(2,1)} %get-tuple-element.8) | data formatting | bytes 1048576
  115.9 1.9 %copy.16 = bf16[1024,256]{1,0:T(8,128)(2,1)} copy(bf16[1024,256]{1,0:T(8,128)(2,1)} %get-tuple-element.9) | data formatting | bytes 1048576
  (1 shorter events, 0.0 us)
where the time goes:
time: 120 us; the launch traced here: 118 us
  Pallas kernels  109 us (91%)
  local copies, waits for them, and re-layouts  6.04 us (5%)
  other arithmetic  1.97 us (2%)
    pallas_call x1, Pallas kernels, per_device(): pl.pallas_call(layer_kernel, out_shape=(result, result), in_specs=[whole]...  109 us
    unnamed x2, local copies, waits for them, and re-layouts  3.74 us

commit v1 on v0

--- a/solution.py
+++ b/solution.py
@@ -52,6 +52,17 @@
     )
 
 
+def to_seq(src, dst, send_sem, recv_sem, place):
+    return pltpu.make_async_remote_copy(
+        src_ref=src,
+        dst_ref=dst,
+        send_sem=send_sem,
+        recv_sem=recv_sem,
+        device_id={"seq": place},
+        device_id_type=MESH,
+    )
+
+
 def rows_of(c):
     return pl.ds(pl.multiple_of(c * CH, CH), CH)
 
@@ -66,20 +77,40 @@
         self.held, self.weight, self.own, self.dims = held, weight, own, dims
         self.part, self.landed, self.relay = part, landed, relay
         self.keep, self.res, self.out = keep, res, out
-        (self.gs, self.gr, self.ts, self.tr, self.ps, self.pr, self.ws, self.wr, self.wo) = sems
+        (self.gs, self.gr, self.ts, self.tr, self.ps, self.pr) = sems[:6]
+        (self.ws, self.wr, self.us, self.ur, self.wo, self.os) = sems[6:]
 
     def weight_copies(self, w_block):
+        core = lax.rem(lax.axis_index("seq"), 2)
         copies = []
         for d in range(1, 4):
-            for k in range(4):
-                src = w_block(block_at(self.a, d, self.r, k))
+            for j in range(2):
+                k = core * 2 + j
                 copies.append(
                     to_device(
-                        src,
+                        w_block(block_at(self.a, d, self.r, k)),
                         self.weight.at[k, d],
-                        self.ws.at[d - 1, k],
-                        self.wr.at[d - 1, k],
+                        self.ws.at[d - 1, j],
+                        self.wr.at[d - 1, j],
                         neighbour(self.a, d),
+                    )
+                )
+        return copies
+
+    def swap_copies(self):
+        place = lax.axis_index("seq")
+        core = lax.rem(place, 2)
+        copies = []
+        for d in range(1, 4):
+            for j in range(2):
+                block = self.weight.at[core * 2 + j, d]
+                copies.append(
+                    to_seq(
+                        block,
+                        block,
+                        self.us.at[d - 1, j],
+                        self.ur.at[d - 1, j],
+                        place + 1 - 2 * core,
                     )
                 )
         return copies
@@ -169,7 +200,13 @@
         total = self.keep[0, rows_of(c)] + (
             self.landed[0, rows_of(c)].astype(f32) + self.landed[1, rows_of(c)].astype(f32)
         )
-        self.out[rows_of(c)] = total.astype(bf16)
+        self.part[0, rows_of(c)] = total.astype(bf16)
+        self.leave(c).start()
+
+    def leave(self, c):
+        return pltpu.make_async_copy(
+            self.part.at[0, rows_of(c)], self.out.at[rows_of(c)], self.os.at[c]
+        )
 
     def drain(self, c):
         self.direct(c, 1).wait_send()
@@ -178,6 +215,7 @@
         self.tie(c).wait_send()
         self.side(c, 1).wait_send()
         self.side(c, 3).wait_send()
+        self.leave(c).wait()
 
 
 def ring_semaphores():
@@ -189,9 +227,12 @@
         dma((NCH,)),
         dma((2, NCH)),
         dma((2, NCH)),
-        dma((3, 4)),
-        dma((3, 4)),
+        dma((3, 2)),
+        dma((3, 2)),
+        dma((3, 2)),
+        dma((3, 2)),
         dma((4,)),
+        dma((NCH,)),
     ]
 
 
@@ -242,17 +283,6 @@
     return jnp.where(condition, 1.0, 0.0).astype(f32)
 
 
-def to_seq(src, dst, send_sem, recv_sem, place):
-    return pltpu.make_async_remote_copy(
-        src_ref=src,
-        dst_ref=dst,
-        send_sem=send_sem,
-        recv_sem=recv_sem,
-        device_id={"seq": place},
-        device_id_type=MESH,
-    )
-
-
 class Carry:
     def __init__(self, earlier, local, state, bufs, sems):
         self.earlier, self.local, self.state = earlier, local, state
@@ -307,7 +337,7 @@
 
 
 def layer_kernel(
-    inputs, cotangent, w_t, w_out, taps, gains, first, second, rows, moves,
+    inputs, cotangent, w_t, w_out, first_any, second_any, moves_any, conv, gains, rows, keep,
     layer_out, input_grad, *scratch,
 ):
     take = list(scratch)
@@ -318,13 +348,14 @@
         return got
 
     fwd_bufs, bwd_bufs = pop(7), pop(7)
-    fwd_sems, bwd_sems = pop(9), pop(9)
+    fwd_sems, bwd_sems = pop(12), pop(12)
     early_bufs, late_bufs = pop(6), pop(6)
     early_sems, late_sems = pop(3), pop(3)
     (xin, cot, weights_t, weights_o) = pop(4)
     (pp, cv, mix, gh, dn, phi_q, phi_k, states, grads, scaled, dconv) = pop(11)
     (state_in, state_out, local_in, local_out, halo_in, halo_out) = pop(6)
-    (x_sem, c_sem, w_sem, o_sem, r_sem, h_sem) = pop(6)
+    (first, second, moves) = pop(3)
+    (x_sem, c_sem, w_sem, o_sem, r_sem, h_sem, k_sem) = pop(7)
 
     tp, place = lax.axis_index("tp"), lax.axis_index("seq")
 
@@ -333,7 +364,7 @@
         return Ring(a, r, held, weight, None, NN, part, landed, relay, keep, res, out, sems)
 
     fwd = ring("x", "y", fwd_bufs, fwd_sems, layer_out)
-    bwd = ring("y", "x", bwd_bufs, bwd_sems, input_grad)
+    bwd = ring("x", "y", bwd_bufs, bwd_sems, input_grad)
     early = Carry(True, local_in, state_in, early_bufs, early_sems)
     later = Carry(False, local_out, state_out, late_bufs, late_sems)
     heads, d_proj = fwd.held.at[0], bwd.held.at[0]
@@ -363,23 +394,10 @@
     def c_load(c):
         return pltpu.make_async_copy(cotangent.at[rows_of(c)], cot.at[rows_of(c)], c_sem.at[c])
 
-    for c in (3, 0, 1, 2):
-        x_load(c).start()
-    o_load = pltpu.make_async_copy(w_out, weights_o, o_sem.at[0])
-    o_load.start()
-    for c in range(NCH):
-        c_load(c).start()
-    res_loads = [
-        pltpu.make_async_copy(inputs.at[:, columns(tp)], fwd.res, r_sem.at[0]),
-        pltpu.make_async_copy(cotangent.at[:, columns(tp)], bwd.res, r_sem.at[1]),
-    ]
-    fwd_own = fwd.own_copies(out_block)
-    for copy in res_loads + fwd_own:
-        copy.start()
-
+    x_load(3).start()
     barrier = pltpu.get_barrier_semaphore()
-    for along in ("x", "y"):
-        for d in (1, 2, 3):
+    for d in (1, 2, 3):
+        for along in ("x", "y"):
             pl.semaphore_signal(
                 barrier, inc=1, device_id={"tp": neighbour(along, d)}, device_id_type=MESH
             )
@@ -388,15 +406,40 @@
             barrier, inc=1, device_id={"seq": lax.rem(place + d, 8)}, device_id_type=MESH
         )
     weights_t[pl.ds(320, 64)] = jnp.zeros((64, weights_t.shape[1]), bf16)
-    pl.semaphore_wait(barrier, 11)
-    fwd_weights = fwd.weight_copies(out_block)
-    for copy in fwd_weights:
-        copy.start()
+    const_loads = [
+        pltpu.make_async_copy(src, dst, k_sem.at[n])
+        for n, (src, dst) in enumerate(
+            ((first_any, first), (second_any, second), (moves_any, moves))
+        )
+    ]
+    o_load = pltpu.make_async_copy(w_out, weights_o, o_sem.at[0])
+    res_loads = [
+        pltpu.make_async_copy(inputs.at[:, columns(tp)], fwd.res, r_sem.at[0]),
+        pltpu.make_async_copy(cotangent.at[:, columns(tp)], bwd.res, r_sem.at[1]),
+    ]
+    fwd_own, bwd_own = fwd.own_copies(out_block), bwd.own_copies(in_block)
+    fwd_weights, bwd_weights = fwd.weight_copies(out_block), bwd.weight_copies(in_block)
+    fwd_swaps, bwd_swaps = fwd.swap_copies(), bwd.swap_copies()
+
+    src = lax.broadcasted_iota(jnp.int32, (320, LANES), 0)
+    dst = lax.broadcasted_iota(jnp.int32, (320, LANES), 1)
+    from_high = jnp.where(dst < 288, dst - 256, jnp.where(dst < 320, dst - 128, -1))
+    source = jnp.where(dst < 128, dst + 32, jnp.where(dst < 256, dst + 64, from_high))
+    taps = lax.dot_general(
+        conv[...],
+        jnp.where(src == source, 1.0, 0.0).astype(f32),
+        NN,
+        precision=lax.Precision.HIGHEST,
+        preferred_element_type=f32,
+    )
+    lane = lax.broadcasted_iota(jnp.int32, (1, HEADS * DV), 1)
+    gain = gains[...] * jnp.where(lane < DV, keep[0].astype(f32), keep[1].astype(f32))
+
     for copy in w_loads:
         copy.wait()
-    bwd_own = bwd.own_copies(in_block)
-    bwd_weights = bwd.weight_copies(in_block)
-    for copy in bwd_weights + bwd_own:
+    for c in (0, 1, 2):
+        x_load(c).start()
+    for copy in const_loads + [o_load] + res_loads + fwd_own + bwd_own:
         copy.start()
 
     ahead = to_seq(
@@ -410,13 +453,19 @@
     def _(i):
         c = lax.rem(i + NCH - 1, NCH)
         x_load(c).wait()
+        c_load(c).start()
         projected = dot(xin[rows_of(c)], weights_t[...], NT).astype(bf16).astype(f32)
         pp[pl.ds(pl.multiple_of(c * CH + 8, 8), CH)] = projected
 
         @pl.when(i == 0)
         def _():
+            pl.semaphore_wait(barrier, 11)
             ahead.start()
-
+            for copy in fwd_weights + bwd_weights:
+                copy.start()
+
+    for copy in const_loads:
+        copy.wait()
     ahead.wait()
     pp[pl.ds(0, 8)] = halo_in[...] * one_if(place > 0)
 
@@ -469,14 +518,11 @@
             early.middle()
 
     o_load.wait()
-    gain = gains[0:1]
 
     @pl.loop(0, NCH)
     def _(c):
         c_load(c).wait()
         gh[rows_of(c)] = dot(cot[rows_of(c)], weights_o[...], NT) * gain
-
-    early.late()
 
     @pl.loop(0, NCH)
     def _(c):
@@ -485,6 +531,7 @@
             a, b = factors(qk, 2 * h)
             phi_q[h, rows_of(c)] = (a * b).astype(bf16)
 
+    early.late()
     early.end()
     local_out[...] = jnp.zeros(local_out.shape, f32)
 
@@ -508,6 +555,10 @@
         fwd.send_own(c)
 
     later.start()
+    for copy in fwd_weights:
+        copy.wait()
+    for copy in fwd_swaps:
+        copy.start()
 
     @pl.loop(0, NCH)
     def _(c):
@@ -540,8 +591,6 @@
 
         fwd.forward(c)
 
-    for copy in fwd_weights + fwd_own + res_loads:
-        copy.wait()
     later.end()
     state_out[...] = state_out[...] + local_out[...]
 
@@ -578,33 +627,46 @@
         def _():
             project_back(c - 1)
 
-        fwd.multiply(c)
-
     behind.wait()
     dconv[pl.ds(NCH * CH, 8)] = halo_out[...] * one_if(place < 7)
     project_back(NCH - 1)
-    for copy in bwd_weights + bwd_own:
+    for copy in bwd_weights:
         copy.wait()
-
-    @pl.loop(0, NCH + 3)
+    for copy in bwd_swaps:
+        copy.start()
+    for copy in fwd_swaps + fwd_own + bwd_own + res_loads:
+        copy.wait()
+
+    @pl.loop(0, NCH)
+    def _(i):
+        fwd.multiply(i)
+        bwd.forward(i)
+
+        @pl.when(i >= 1)
+        def _():
+            fwd.relayed(i - 1)
+
+    for copy in bwd_swaps:
+        copy.wait()
+
+    @pl.loop(0, NCH + 2)
     def _(i):
         @pl.when(i < NCH)
         def _():
-            bwd.forward(i)
-            fwd.relayed(i)
+            bwd.multiply(i)
+
+        @pl.when(i == 0)
+        def _():
+            fwd.relayed(NCH - 1)
 
         @pl.when((i >= 1) & (i < NCH + 1))
         def _():
-            bwd.multiply(i - 1)
-
-        @pl.when((i >= 2) & (i < NCH + 2))
-        def _():
-            bwd.relayed(i - 2)
-            fwd.finish(i - 2)
-
-        @pl.when(i >= 3)
-        def _():
-            bwd.finish(i - 3)
+            bwd.relayed(i - 1)
+            fwd.finish(i - 1)
+
+        @pl.when(i >= 2)
+        def _():
+            bwd.finish(i - 2)
 
     @pl.loop(0, NCH)
     def _(c):
@@ -615,28 +677,47 @@
     later.drain()
 
 
-def permuted(array):
-    parts = [array[..., 32:160], array[..., 192:320], array[..., 0:32], array[..., 160:192]]
-    return jnp.concatenate(parts + [jnp.zeros(array.shape[:-1] + (64,), array.dtype)], -1)
+def settle_kernel(first, second, first_out, second_out, held, in_sem, out_sem):
+    pairs = ((first, first_out), (second, second_out))
+    ins = [pltpu.make_async_copy(p[0], held.at[n], in_sem.at[n]) for n, p in enumerate(pairs)]
+    outs = [pltpu.make_async_copy(held.at[n], p[1], out_sem.at[n]) for n, p in enumerate(pairs)]
+    for copy in ins:
+        copy.start()
+    for n in range(2):
+        ins[n].wait()
+        outs[n].start()
+    for copy in outs:
+        copy.wait()
+
+
+def settle(first, second):
+    whole = pl.BlockSpec(memory_space=pl.ANY)
+    result = jax.ShapeDtypeStruct(first.shape, first.dtype)
+    dma = pltpu.SemaphoreType.DMA
+    return pl.pallas_call(
+        settle_kernel,
+        out_shape=(result, result),
+        in_specs=[whole] * 2,
+        out_specs=(whole, whole),
+        scratch_shapes=[pltpu.VMEM((2,) + first.shape, first.dtype), dma((2,)), dma((2,))],
+    )(first, second)
 
 
 def per_device(inputs, cotangent, w_in, conv_w, norm_gain, w_out, keep_flags):
     count, width = inputs.shape
-    taps = jnp.pad(permuted(conv_w), ((0, 5), (0, 0)))
-    gains = (norm_gain.reshape(HEADS, DV) * keep_flags.astype(f32)[:, None]).reshape(1, HEADS * DV)
     first, second, rows, moves = selectors()
-    consts = [jnp.asarray(first, bf16), jnp.asarray(second, bf16), jnp.asarray(rows), jnp.asarray(moves, bf16)]
+    consts = [jnp.asarray(part, bf16) for part in (first, second, moves)]
     whole, near = pl.BlockSpec(memory_space=pl.ANY), pl.BlockSpec(memory_space=pltpu.VMEM)
     result = jax.ShapeDtypeStruct((count, 256), bf16)
     dma = pltpu.SemaphoreType.DMA
     state = (DV, EXP)
     carry_bufs = [pltpu.VMEM((n,) + state if n > 1 else state, bf16) for n in (1, 1, 1, 3, 1, 1)]
     carry_sems = [dma((4,)), dma((3,)), dma((3,))]
-    return pl.pallas_call(
+    results = pl.pallas_call(
         layer_kernel,
         out_shape=(result, result),
-        in_specs=[whole] * 4 + [near] * 6,
-        out_specs=(near, near),
+        in_specs=[whole] * 7 + [near] * 3 + [pl.BlockSpec(memory_space=pltpu.SMEM)],
+        out_specs=(whole, whole),
         scratch_shapes=ring_buffers(count, 256, (256, 256))
         + ring_buffers(count, 320, (320, 256))
         + ring_semaphores()
@@ -667,17 +748,32 @@
             pltpu.VMEM((HEADS,) + state, f32),
             pltpu.VMEM((8, LANES), f32),
             pltpu.VMEM((8, LANES), f32),
+            pltpu.VMEM((4, 128, EXP), bf16),
+            pltpu.VMEM((4, 128, EXP), bf16),
+            pltpu.VMEM((4, 128, 128), bf16),
             dma((NCH,)),
             dma((NCH,)),
             dma((4,)),
             dma((1,)),
             dma((2,)),
             dma((4,)),
+            dma((3,)),
         ],
         compiler_params=pltpu.CompilerParams(
             collective_id=0, has_side_effects=True, vmem_limit_bytes=62 << 20
         ),
-    )(inputs, cotangent, w_in.T, w_out, taps, gains, *consts)
+    )(
+        inputs,
+        cotangent,
+        w_in.T,
+        w_out,
+        *consts,
+        conv_w,
+        norm_gain.reshape(1, HEADS * DV),
+        jnp.asarray(rows),
+        keep_flags,
+    )
+    return settle(*results)
 
 
 def solution(mesh):

time: 120 us -> 101 us (0.84); the launches traced: 118 us -> 101 us
  Pallas kernels: 109 us -> 100 us
  local copies, waits for them, and re-layouts: 6.04 us -> 0 us
  other arithmetic: 1.97 us -> 0 us
    pallas_call x1, Pallas kernels: 109 us -> 97.9 us  [per_device(): pl.pallas_call(layer_kernel, out_shape=(result, result), in_specs=[whole]...]
    unnamed x2 -> x0, local copies, waits for them, and re-layouts: 3.74 us -> none
    pallas_call x0 -> x1, Pallas kernels: none -> 2.04 us  [settle(): pl.pallas_call(settle_kernel, out_shape=(result, result), in_specs=[whole...]
    slice x2 -> x0, local copies, waits for them, and re-layouts: 1.6 us -> none  [the longest x1 0.83 us: permuted(): array[..., 192:320]]
    mul x1 -> x0, other arithmetic: 1.31 us -> none  [per_device(): norm_gain.reshape(HEADS, DV) * keep_flags.astype(f32)[:, None]]
where the time goes in v1:
time: 101 us
  Pallas kernels  100 us (99%)
    pallas_call x1, Pallas kernels, per_device(): pl.pallas_call(layer_kernel, out_shape=(result, result), in_specs=[whole]...  97.9 us
    pallas_call x1, Pallas kernels, settle(): pl.pallas_call(settle_kernel, out_shape=(result, result), in_specs=[whole...  2.04 us

profile of v1, /device:TPU:1, one launch (start us, length us, event | category | flops | bytes accessed | tf_op | source)
XLA Modules:
  0.0 100.6 jit_solution(7088818880856131683)
XLA Ops:
  0.6 97.9 %shard_map.122 = (bf16[1024,256]{1,0:T(8,128)(2,1)}, bf16[1024,256]{1,0:T(8,128)(2,1)}) custom-call(bf16[1024,4096]{1,0:T(8,128)(2,1)} %inputs.1, bf16[1024,4096]{1,0:T(8,128)(2,1)} %cotangent.1, bf16[320,4096]{1,0:T(8,128)(2,1)} %bitcast.2, bf16[256,4096]{1,0:T(8,128)(2,1)} %w_out.1, bf16[4,128,256]{2,1,0:T(8,128)(2,1)} %constant.8.clone.first_any, ...), custom_call_target="tpu_custom_call" | custom-call | tf_op jit(solution)/shard_map/pallas_call | solution.py:716
  98.6 2.0 %shard_map.123 = (bf16[1024,256]{1,0:T(8,128)(2,1)}, bf16[1024,256]{1,0:T(8,128)(2,1)}) custom-call(bf16[1024,256]{1,0:T(8,128)(2,1)} %get-tuple-element.4.first, bf16[1024,256]{1,0:T(8,128)(2,1)} %get-tuple-element.5.second), custom_call_target="tpu_custom_call" | custom-call | tf_op jit(solution)/shard_map/pallas_call | solution.py:697

commit v2 on v1

--- a/solution.py
+++ b/solution.py
@@ -63,8 +63,12 @@
     )
 
 
-def rows_of(c):
-    return pl.ds(pl.multiple_of(c * CH, CH), CH)
+def dot(a, b, dims=NN):
+    return lax.dot_general(a, b, dims, preferred_element_type=f32)
+
+
+def rows_of(c, size=CH):
+    return pl.ds(pl.multiple_of(c * size, size), size)
 
 
 def way(c):
@@ -72,83 +76,47 @@
 
 
 class Ring:
-    def __init__(self, a, r, held, weight, own, dims, part, landed, relay, keep, res, out, sems):
-        self.a, self.r = a, r
-        self.held, self.weight, self.own, self.dims = held, weight, own, dims
+    def __init__(self, a, r, streams, weight, part, landed, relay, keep, res, out, sems):
+        self.a, self.r, self.streams, self.weight = a, r, streams, weight
         self.part, self.landed, self.relay = part, landed, relay
         self.keep, self.res, self.out = keep, res, out
-        (self.gs, self.gr, self.ts, self.tr, self.ps, self.pr) = sems[:6]
-        (self.ws, self.wr, self.us, self.ur, self.wo, self.os) = sems[6:]
-
-    def weight_copies(self, w_block):
-        core = lax.rem(lax.axis_index("seq"), 2)
-        copies = []
-        for d in range(1, 4):
-            for j in range(2):
-                k = core * 2 + j
-                copies.append(
-                    to_device(
-                        w_block(block_at(self.a, d, self.r, k)),
-                        self.weight.at[k, d],
-                        self.ws.at[d - 1, j],
-                        self.wr.at[d - 1, j],
-                        neighbour(self.a, d),
-                    )
-                )
-        return copies
-
-    def swap_copies(self):
-        place = lax.axis_index("seq")
-        core = lax.rem(place, 2)
-        copies = []
-        for d in range(1, 4):
-            for j in range(2):
-                block = self.weight.at[core * 2 + j, d]
-                copies.append(
-                    to_seq(
-                        block,
-                        block,
-                        self.us.at[d - 1, j],
-                        self.ur.at[d - 1, j],
-                        place + 1 - 2 * core,
-                    )
-                )
-        return copies
-
-    def own_copies(self, w_block):
+        (self.ts, self.tr, self.ps, self.pr, self.os) = sems
+
+    def direct(self, c, d):
         return [
-            pltpu.make_async_copy(
-                w_block(block_at(self.a, 0, self.r, k)), self.weight.at[k, 0], self.wo.at[k]
+            to_device(
+                held.at[0, rows_of(c, size)],
+                held.at[d, rows_of(c, size)],
+                send.at[d - 1, c],
+                recv.at[d - 1, c],
+                neighbour(self.a, d),
             )
-            for k in range(4)
+            for held, size, send, recv in self.streams
         ]
 
-    def direct(self, c, d):
-        return to_device(
-            self.held.at[0, rows_of(c)],
-            self.held.at[d, rows_of(c)],
-            self.gs.at[d - 1, c],
-            self.gr.at[d - 1, c],
-            neighbour(self.a, d),
-        )
-
     def passed_on(self, c):
-        return to_device(
-            self.held.at[way(c), rows_of(c)],
-            self.held.at[2, rows_of(c)],
-            self.gs.at[1, c],
-            self.gr.at[1, c],
-            neighbour(self.a, way(c)),
-        )
+        return [
+            to_device(
+                held.at[way(c), rows_of(c, size)],
+                held.at[2, rows_of(c, size)],
+                send.at[1, c],
+                recv.at[1, c],
+                neighbour(self.a, way(c)),
+            )
+            for held, size, send, recv in self.streams
+        ]
 
     def send_own(self, c):
-        self.direct(c, 1).start()
-        self.direct(c, 3).start()
+        for d in (1, 3):
+            for copy in self.direct(c, d):
+                copy.start()
 
     def forward(self, c):
-        self.direct(c, 1).wait_recv()
-        self.direct(c, 3).wait_recv()
-        self.passed_on(c).start()
+        for d in (1, 3):
+            for copy in self.direct(c, d):
+                copy.wait_recv()
+        for copy in self.passed_on(c):
+            copy.start()
 
     def tie(self, c):
         return to_device(
@@ -168,17 +136,21 @@
             neighbour(self.r, d),
         )
 
+    def prepare(self, c):
+        pass
+
     def product(self, c, k):
+        held = self.streams[0][0]
         total = None
         for o in range(4):
-            term = lax.dot_general(
-                self.held[o, rows_of(c)], self.weight[k, o], self.dims, preferred_element_type=f32
-            )
+            term = dot(held[o, rows_of(c)], self.weight[k, o])
             total = term if total is None else total + term
         return total
 
     def multiply(self, c):
-        self.passed_on(c).wait_recv()
+        for copy in self.passed_on(c):
+            copy.wait_recv()
+        self.prepare(c)
         near, far = way(c), 4 - way(c)
         self.part[2, rows_of(c)] = self.product(c, 2).astype(bf16)
         self.tie(c).start()
@@ -209,37 +181,39 @@
         )
 
     def drain(self, c):
-        self.direct(c, 1).wait_send()
-        self.direct(c, 3).wait_send()
-        self.passed_on(c).wait_send()
+        for copy in self.direct(c, 1) + self.direct(c, 3) + self.passed_on(c):
+            copy.wait_send()
         self.tie(c).wait_send()
         self.side(c, 1).wait_send()
         self.side(c, 3).wait_send()
         self.leave(c).wait()
 
 
+class SplitRing(Ring):
+    def prepare(self, c):
+        packed = self.streams[1][0]
+        low = lax.broadcasted_iota(jnp.int32, (CH // 2, 128), 1) < 64
+        for pair in range(2):
+            one = packed[2 * pair, rows_of(c, CH // 2)].astype(f32)
+            two = packed[2 * pair + 1, rows_of(c, CH // 2)].astype(f32)
+            top = jnp.where(low, one, pltpu.roll(two, 64, 1))
+            bottom = jnp.where(low, pltpu.roll(one, 64, 1), two)
+            lanes = slice(pair * 128, pair * 128 + 128)
+            self.flat[0 : CH // 2, lanes] = top.astype(bf16)
+            self.flat[CH // 2 : CH, lanes] = bottom.astype(bf16)
+
+    def product(self, c, k):
+        return super().product(c, k) + dot(self.flat[...], self.weight_qk[k].reshape(256, 256))
+
+
 def ring_semaphores():
     dma = pltpu.SemaphoreType.DMA
+    return [dma((NCH,)), dma((NCH,)), dma((2, NCH)), dma((2, NCH)), dma((NCH,))]
+
+
+def ring_buffers(rows):
     return [
-        dma((3, NCH)),
-        dma((3, NCH)),
-        dma((NCH,)),
-        dma((NCH,)),
-        dma((2, NCH)),
-        dma((2, NCH)),
-        dma((3, 2)),
-        dma((3, 2)),
-        dma((3, 2)),
-        dma((3, 2)),
-        dma((4,)),
-        dma((NCH,)),
-    ]
-
-
-def ring_buffers(rows, width, weight_shape):
-    return [
-        pltpu.VMEM((4, rows, width), bf16),
-        pltpu.VMEM((4, 4) + weight_shape, bf16),
+        pltpu.VMEM((4, 4, 256, 256), bf16),
         pltpu.VMEM((4, rows, 256), bf16),
         pltpu.VMEM((2, rows, 256), bf16),
         pltpu.VMEM((rows, 256), bf16),
@@ -275,10 +249,6 @@
     return first, second, rows, moves
 
 
-def dot(a, b, dims=NN):
-    return lax.dot_general(a, b, dims, preferred_element_type=f32)
-
-
 def one_if(condition):
     return jnp.where(condition, 1.0, 0.0).astype(f32)
 
@@ -347,8 +317,12 @@
         del take[:n]
         return got
 
-    fwd_bufs, bwd_bufs = pop(7), pop(7)
-    fwd_sems, bwd_sems = pop(12), pop(12)
+    fwd_bufs, bwd_bufs = pop(6), pop(6)
+    fwd_sems, bwd_sems = pop(5), pop(5)
+    (held_h, held_v, held_qk, weight_qk, flat, saved_w, saved_l, moved_q) = pop(8)
+    (gs_h, gr_h, gs_v, gr_v, gs_q, gr_q) = pop(6)
+    (ws, wr, us, ur, w_own, q_own) = pop(6)
+    (fs, fr, zcs, zcr, ss, sr) = pop(6)
     early_bufs, late_bufs = pop(6), pop(6)
     early_sems, late_sems = pop(3), pop(3)
     (xin, cot, weights_t, weights_o) = pop(4)
@@ -359,15 +333,14 @@
 
     tp, place = lax.axis_index("tp"), lax.axis_index("seq")
 
-    def ring(a, r, bufs, sems, out):
-        held, weight, part, landed, relay, keep, res = bufs
-        return Ring(a, r, held, weight, None, NN, part, landed, relay, keep, res, out, sems)
-
-    fwd = ring("x", "y", fwd_bufs, fwd_sems, layer_out)
-    bwd = ring("x", "y", bwd_bufs, bwd_sems, input_grad)
+    core, z = lax.rem(place, 2), lax.div(place, 2)
+    fwd = Ring("x", "y", [(held_h, CH, gs_h, gr_h)], *fwd_bufs, layer_out, fwd_sems)
+    streams = [(held_v, CH, gs_v, gr_v), (held_qk, CH // 2, gs_q, gr_q)]
+    bwd = SplitRing("x", "y", streams, *bwd_bufs, input_grad, bwd_sems)
+    bwd.flat, bwd.weight_qk = flat, weight_qk
     early = Carry(True, local_in, state_in, early_bufs, early_sems)
     later = Carry(False, local_out, state_out, late_bufs, late_sems)
-    heads, d_proj = fwd.held.at[0], bwd.held.at[0]
+    heads = held_h.at[0]
 
     def columns(t):
         return pl.ds(pl.multiple_of(t * 256, 256), 256)
@@ -375,8 +348,54 @@
     def out_block(t):
         return w_out.at[:, columns(t)]
 
-    def in_block(t):
-        return weights_t.at[pl.ds(0, 320), columns(t)]
+    def swap_device():
+        return place + 1 - 2 * core
+
+    fwd_weights, fwd_swaps = [], []
+    for d in (1, 2, 3):
+        for j in range(2):
+            k = core * 2 + j
+            block = fwd.weight.at[k, d]
+            at = (d - 1, j)
+            fwd_weights.append(
+                to_device(
+                    out_block(block_at("x", d, "y", k)), block, ws.at[at], wr.at[at], neighbour("x", d)
+                )
+            )
+            fwd_swaps.append(to_seq(block, block, us.at[at], ur.at[at], swap_device()))
+
+    sides = ((bwd.weight, 128, 0), (weight_qk, 32, 256))
+    bwd_weights, spreads, bwd_swaps = [], [], []
+    for n, (array, size, start) in enumerate(sides):
+        half = rows_of(core, size)
+        theirs = pl.ds(pl.multiple_of(start + core * size, size), size)
+        for d in (1, 2, 3):
+            at = (n, d - 1)
+            bwd_weights.append(
+                to_device(
+                    weights_t.at[theirs, columns(block_at("x", d, "y", z))],
+                    array.at[z, d, half],
+                    fs.at[at],
+                    fr.at[at],
+                    neighbour("x", d),
+                )
+            )
+            mine = array.at[z, pl.ds(1, 3), half]
+            there = lax.rem(z + d, 4) * 2 + core
+            spreads.append(to_seq(mine, mine, zcs.at[at], zcr.at[at], there))
+        ours = array.at[:, pl.ds(1, 3), half]
+        bwd_swaps.append(to_seq(ours, ours, ss.at[n], sr.at[n], swap_device()))
+
+    fwd_own, bwd_own = [], []
+    for k in range(4):
+        t = block_at("x", 0, "y", k)
+        fwd_own.append(pltpu.make_async_copy(out_block(t), fwd.weight.at[k, 0], w_own.at[0, k]))
+        for n, (array, size, start) in enumerate(sides):
+            bwd_own.append(
+                pltpu.make_async_copy(
+                    weights_t.at[pl.ds(start, 2 * size), columns(t)], array.at[k, 0], q_own.at[n, k]
+                )
+            )
 
     pieces = ((32, 128, 0), (192, 128, 128), (0, 32, 256), (160, 32, 288))
     w_loads = [
@@ -417,10 +436,6 @@
         pltpu.make_async_copy(inputs.at[:, columns(tp)], fwd.res, r_sem.at[0]),
         pltpu.make_async_copy(cotangent.at[:, columns(tp)], bwd.res, r_sem.at[1]),
     ]
-    fwd_own, bwd_own = fwd.own_copies(out_block), bwd.own_copies(in_block)
-    fwd_weights, bwd_weights = fwd.weight_copies(out_block), bwd.weight_copies(in_block)
-    fwd_swaps, bwd_swaps = fwd.swap_copies(), bwd.swap_copies()
-
     src = lax.broadcasted_iota(jnp.int32, (320, LANES), 0)
     dst = lax.broadcasted_iota(jnp.int32, (320, LANES), 1)
     from_high = jnp.where(dst < 288, dst - 256, jnp.where(dst < 320, dst - 128, -1))
@@ -461,7 +476,7 @@
         def _():
             pl.semaphore_wait(barrier, 11)
             ahead.start()
-            for copy in fwd_weights + bwd_weights:
+            for copy in bwd_weights + fwd_weights:
                 copy.start()
 
     for copy in const_loads:
@@ -509,9 +524,13 @@
     def _(c):
         qk = qk_of(c)
         for h in range(HEADS):
-            logits = dot(dot(qk, moves[2 * h]).astype(bf16), qk, NT) * 0.25
-            weight = jnp.where(causal, 1.0 + logits + 0.5 * logits * logits, 0.0)
-            mix[rows_of(c), lanes(h)] = dot(weight.astype(bf16), cv[rows_of(c), lanes(h)])
+            moved = dot(qk, moves[2 * h]).astype(bf16)
+            moved_q[h, rows_of(c)] = moved
+            logits = dot(moved, qk, NT) * 0.25
+            weight = jnp.where(causal, 1.0 + logits + 0.5 * logits * logits, 0.0).astype(bf16)
+            saved_w[h, rows_of(c)] = weight
+            saved_l[h, rows_of(c)] = jnp.where(causal, 0.25 + 0.25 * logits, 0.0)
+            mix[rows_of(c), lanes(h)] = dot(weight, cv[rows_of(c), lanes(h)])
 
         @pl.when(c == 1)
         def _():
@@ -532,6 +551,10 @@
             phi_q[h, rows_of(c)] = (a * b).astype(bf16)
 
     early.late()
+    for copy in bwd_weights:
+        copy.wait()
+    for copy in spreads:
+        copy.start()
     early.end()
     local_out[...] = jnp.zeros(local_out.shape, f32)
 
@@ -565,16 +588,12 @@
         qk = qk_of(c)
         d_qk = jnp.zeros((CH, 128), f32)
         for h in range(HEADS):
-            moved = dot(qk, moves[2 * h]).astype(bf16)
-            logits = dot(moved, qk, NT) * 0.25
-            weight = jnp.where(causal, 1.0 + logits + 0.5 * logits * logits, 0.0)
             rounded = dn[rows_of(c), lanes(h)]
-            dconv[rows_of(c), lanes(h)] = dot(weight.astype(bf16), rounded, TN)
+            dconv[rows_of(c), lanes(h)] = dot(saved_w[h, rows_of(c)], rounded, TN)
             d_weight = dot(rounded, cv[rows_of(c), lanes(h)], NT)
-            d_logits = jnp.where(causal, d_weight * (1.0 + logits), 0.0) * 0.25
-            d_logits = d_logits.astype(bf16)
+            d_logits = (d_weight * saved_l[h, rows_of(c)]).astype(bf16)
             d_qk = d_qk + dot(d_logits, dot(qk, moves[2 * h + 1]).astype(bf16))
-            d_qk = d_qk + dot(d_logits, moved, TN)
+            d_qk = d_qk + dot(d_logits, moved_q[h, rows_of(c)], TN)
             a, b = factors(qk, 2 * h)
             d_phi = dot(rounded, scaled[c, h])
             d_qk = d_qk + dot((d_phi * b).astype(bf16), first[2 * h], NT)
@@ -599,8 +618,9 @@
         mixed = t0 * window[:CH] + (
             t1 * pltpu.roll(window, CH + 7, 0)[:CH] + t2 * pltpu.roll(window, CH + 6, 0)[:CH]
         )
-        d_proj[rows_of(c)] = mixed[:, :320].astype(bf16)
-        bwd.send_own(c)
+        held_v[0, rows_of(c)] = mixed[:, : 2 * DV].astype(bf16)
+        packed = mixed[: CH // 2, 2 * DV :] + pltpu.roll(mixed[CH // 2 :, 2 * DV :], 64, 1)
+        held_qk[0, rows_of(c, CH // 2)] = packed.astype(bf16)
 
     @pl.loop(0, NCH)
     def _(c):
@@ -627,46 +647,52 @@
         def _():
             project_back(c - 1)
 
+        @pl.when((c == 1) | (c == 2))
+        def _():
+            bwd.send_own(c - 1)
+
     behind.wait()
     dconv[pl.ds(NCH * CH, 8)] = halo_out[...] * one_if(place < 7)
     project_back(NCH - 1)
-    for copy in bwd_weights:
-        copy.wait()
-    for copy in bwd_swaps:
-        copy.start()
     for copy in fwd_swaps + fwd_own + bwd_own + res_loads:
         copy.wait()
 
-    @pl.loop(0, NCH)
+    @pl.loop(0, NCH + 3)
     def _(i):
-        fwd.multiply(i)
-        bwd.forward(i)
-
-        @pl.when(i >= 1)
+        @pl.when(i == 1)
+        def _():
+            for copy in spreads:
+                copy.wait()
+            for copy in bwd_swaps:
+                copy.start()
+
+        @pl.when(i < NCH)
+        def _():
+            fwd.multiply(i)
+            bwd.forward(i)
+
+        @pl.when(i < NCH - 2)
+        def _():
+            bwd.send_own(i + 2)
+
+        @pl.when(i == 1)
+        def _():
+            for copy in bwd_swaps:
+                copy.wait()
+
+        @pl.when((i >= 1) & (i < NCH + 1))
         def _():
             fwd.relayed(i - 1)
-
-    for copy in bwd_swaps:
-        copy.wait()
-
-    @pl.loop(0, NCH + 2)
-    def _(i):
-        @pl.when(i < NCH)
-        def _():
-            bwd.multiply(i)
-
-        @pl.when(i == 0)
-        def _():
-            fwd.relayed(NCH - 1)
-
-        @pl.when((i >= 1) & (i < NCH + 1))
-        def _():
-            bwd.relayed(i - 1)
-            fwd.finish(i - 1)
-
-        @pl.when(i >= 2)
-        def _():
-            bwd.finish(i - 2)
+            bwd.multiply(i - 1)
+
+        @pl.when((i >= 2) & (i < NCH + 2))
+        def _():
+            bwd.relayed(i - 2)
+            fwd.finish(i - 2)
+
+        @pl.when(i >= 3)
+        def _():
+            bwd.finish(i - 3)
 
     @pl.loop(0, NCH)
     def _(c):
@@ -718,10 +744,25 @@
         out_shape=(result, result),
         in_specs=[whole] * 7 + [near] * 3 + [pl.BlockSpec(memory_space=pltpu.SMEM)],
         out_specs=(whole, whole),
-        scratch_shapes=ring_buffers(count, 256, (256, 256))
-        + ring_buffers(count, 320, (320, 256))
+        scratch_shapes=ring_buffers(count)
+        + ring_buffers(count)
         + ring_semaphores()
         + ring_semaphores()
+        + [
+            pltpu.VMEM((4, count, 256), bf16),
+            pltpu.VMEM((4, count, 256), bf16),
+            pltpu.VMEM((4, count // 2, 128), bf16),
+            pltpu.VMEM((4, 4, 64, 256), bf16),
+            pltpu.VMEM((CH, 256), bf16),
+            pltpu.VMEM((HEADS, count, CH), bf16),
+            pltpu.VMEM((HEADS, count, CH), f32),
+            pltpu.VMEM((HEADS, count, 128), bf16),
+        ]
+        + [dma((3, NCH))] * 6
+        + [dma((3, 2))] * 4
+        + [dma((1, 4)), dma((2, 4))]
+        + [dma((2, 3))] * 4
+        + [dma((2,))] * 2
         + carry_bufs
         + carry_bufs
         + carry_sems

time: 101 us -> 92.6 us (0.917)
  Pallas kernels: 100 us -> 91.8 us
    pallas_call x1, Pallas kernels: 97.9 us -> 89.8 us  [per_device(): pl.pallas_call(layer_kernel, out_shape=(result, result), in_specs=[whole]...]
where the time goes in v2:
time: 92.6 us; the launch traced here: 92.5 us
  Pallas kernels  91.8 us (99%)
    pallas_call x1, Pallas kernels, per_device(): pl.pallas_call(layer_kernel, out_shape=(result, result), in_specs=[whole]...  89.8 us
    pallas_call x1, Pallas kernels, settle(): pl.pallas_call(settle_kernel, out_shape=(result, result), in_specs=[whole...  2.04 us

profile of v2, /device:TPU:1, one launch (start us, length us, event | category | flops | bytes accessed | tf_op | source)
XLA Modules:
  0.0 92.5 jit_solution(3302415141378545811)
XLA Ops:
  0.6 89.8 %shard_map.122 = (bf16[1024,256]{1,0:T(8,128)(2,1)}, bf16[1024,256]{1,0:T(8,128)(2,1)}) custom-call(bf16[1024,4096]{1,0:T(8,128)(2,1)} %inputs.1, bf16[1024,4096]{1,0:T(8,128)(2,1)} %cotangent.1, bf16[320,4096]{1,0:T(8,128)(2,1)} %bitcast.2, bf16[256,4096]{1,0:T(8,128)(2,1)} %w_out.1, bf16[4,128,256]{2,1,0:T(8,128)(2,1)} %constant.8.clone.first_any, ...), custom_call_target="tpu_custom_call" | custom-call | tf_op jit(solution)/shard_map/pallas_call | solution.py:742
  90.4 2.0 %shard_map.123 = (bf16[1024,256]{1,0:T(8,128)(2,1)}, bf16[1024,256]{1,0:T(8,128)(2,1)}) custom-call(bf16[1024,256]{1,0:T(8,128)(2,1)} %get-tuple-element.4.first, bf16[1024,256]{1,0:T(8,128)(2,1)} %get-tuple-element.5.second), custom_call_target="tpu_custom_call" | custom-call | tf_op jit(solution)/shard_map/pallas_call | solution.py:723

commit v3 on v2

--- a/solution.py
+++ b/solution.py
@@ -76,11 +76,20 @@
 
 
 class Ring:
-    def __init__(self, a, r, streams, weight, part, landed, relay, keep, res, out, sems):
-        self.a, self.r, self.streams, self.weight = a, r, streams, weight
+    def __init__(self, flip, streams, weight, part, landed, relay, keep, res, out, sems):
+        self.flip, self.streams, self.weight = flip, streams, weight
         self.part, self.landed, self.relay = part, landed, relay
         self.keep, self.res, self.out = keep, res, out
         (self.ts, self.tr, self.ps, self.pr, self.os) = sems
+
+    def turn(self, c):
+        return lax.rem(c + self.flip, 2)
+
+    def gather_to(self, c, d):
+        return jnp.where(self.turn(c) == 0, neighbour("x", d), neighbour("y", d))
+
+    def scatter_to(self, c, d):
+        return jnp.where(self.turn(c) == 0, neighbour("y", d), neighbour("x", d))
 
     def direct(self, c, d):
         return [
@@ -89,7 +98,7 @@
                 held.at[d, rows_of(c, size)],
                 send.at[d - 1, c],
                 recv.at[d - 1, c],
-                neighbour(self.a, d),
+                self.gather_to(c, d),
             )
             for held, size, send, recv in self.streams
         ]
@@ -101,7 +110,7 @@
                 held.at[2, rows_of(c, size)],
                 send.at[1, c],
                 recv.at[1, c],
-                neighbour(self.a, way(c)),
+                self.gather_to(c, way(c)),
             )
             for held, size, send, recv in self.streams
         ]
@@ -124,7 +133,7 @@
             self.relay.at[rows_of(c)],
             self.ts.at[c],
             self.tr.at[c],
-            neighbour(self.r, way(c)),
+            self.scatter_to(c, way(c)),
         )
 
     def side(self, c, d):
@@ -133,7 +142,7 @@
             self.landed.at[d // 2, rows_of(c)],
             self.ps.at[d // 2, c],
             self.pr.at[d // 2, c],
-            neighbour(self.r, d),
+            self.scatter_to(c, d),
         )
 
     def prepare(self, c):
@@ -143,9 +152,23 @@
         held = self.streams[0][0]
         total = None
         for o in range(4):
-            term = dot(held[o, rows_of(c)], self.weight[k, o])
+            term = dot(held[o, rows_of(c)], self.weight[self.turn(c), k, o])
             total = term if total is None else total + term
         return total
+
+    def compute(self, c):
+        for copy in self.passed_on(c):
+            copy.wait_recv()
+        self.prepare(c)
+        near, far = way(c), 4 - way(c)
+        self.part[2, rows_of(c)] = self.product(c, 2).astype(bf16)
+        self.part[far, rows_of(c)] = self.product(c, far).astype(bf16)
+        self.keep[1, rows_of(c)] = self.product(c, near)
+        self.keep[0, rows_of(c)] = self.product(c, 0) + self.res[rows_of(c)].astype(f32)
+
+    def send(self, c):
+        self.tie(c).start()
+        self.side(c, 4 - way(c)).start()
 
     def multiply(self, c):
         for copy in self.passed_on(c):
@@ -154,9 +177,9 @@
         near, far = way(c), 4 - way(c)
         self.part[2, rows_of(c)] = self.product(c, 2).astype(bf16)
         self.tie(c).start()
+        self.keep[1, rows_of(c)] = self.product(c, near)
         self.part[far, rows_of(c)] = self.product(c, far).astype(bf16)
         self.side(c, far).start()
-        self.keep[1, rows_of(c)] = self.product(c, near)
         self.keep[0, rows_of(c)] = self.product(c, 0) + self.res[rows_of(c)].astype(f32)
 
     def relayed(self, c):
@@ -203,7 +226,7 @@
             self.flat[CH // 2 : CH, lanes] = bottom.astype(bf16)
 
     def product(self, c, k):
-        return super().product(c, k) + dot(self.flat[...], self.weight_qk[k].reshape(256, 256))
+        return super().product(c, k) + dot(self.flat[...], self.weight_qk[self.turn(c), k].reshape(256, 256))
 
 
 def ring_semaphores():
@@ -213,7 +236,7 @@
 
 def ring_buffers(rows):
     return [
-        pltpu.VMEM((4, 4, 256, 256), bf16),
+        pltpu.VMEM((2, 4, 4, 256, 256), bf16),
         pltpu.VMEM((4, rows, 256), bf16),
         pltpu.VMEM((2, rows, 256), bf16),
         pltpu.VMEM((rows, 256), bf16),
@@ -253,6 +276,21 @@
     return jnp.where(condition, 1.0, 0.0).astype(f32)
 
 
+def packed_state(state):
+    rest = state[:32, DV:]
+    for g in range(1, 4):
+        rest = rest + pltpu.roll(state[32 * g : 32 * g + 32, DV:], 32 * g, 1)
+    return jnp.concatenate([state[:, :DV], rest], 0)
+
+
+def whole_state(packed):
+    low = lax.broadcasted_iota(jnp.int32, (32, DV), 1) < 32
+    rest = packed[DV:]
+    parts = [rest] + [pltpu.roll(rest, DV - 32 * g, 1) for g in range(1, 4)]
+    parts = [jnp.where(low, part, 0.0) for part in parts]
+    return jnp.concatenate([packed[:DV], jnp.concatenate(parts, 0)], 1)
+
+
 class Carry:
     def __init__(self, earlier, local, state, bufs, sems):
         self.earlier, self.local, self.state = earlier, local, state
@@ -275,12 +313,12 @@
         )
 
     def start(self):
-        self.sa[...] = self.local[1 - self.core].astype(bf16)
+        self.sa[...] = packed_state(self.local[1 - self.core]).astype(bf16)
         self.swap().start()
 
     def middle(self):
         self.swap().wait_recv()
-        self.sb[...] = (self.local[self.core] + self.ra[...].astype(f32)).astype(bf16)
+        self.sb[...] = (packed_state(self.local[self.core]) + self.ra[...].astype(f32)).astype(bf16)
         for step in (1, 2, 3):
             self.along(step).start()
 
@@ -291,13 +329,14 @@
             counts = one_if(self.z >= step if self.earlier else self.z < step)
             total = total + self.rb[step - 1].astype(f32) * counts
         takes = self.core if self.earlier else 1 - self.core
-        self.sc[...] = (total + self.local[self.core] * one_if(takes == 0)).astype(bf16)
+        own = packed_state(self.local[self.core]) * one_if(takes == 0)
+        self.sc[...] = (total + own).astype(bf16)
         self.give().start()
-        self.state[self.core] = total + self.ra[...].astype(f32) * one_if(takes == 1)
+        self.state[self.core] = whole_state(total + self.ra[...].astype(f32) * one_if(takes == 1))
 
     def end(self):
         self.give().wait_recv()
-        self.state[1 - self.core] = self.rc[...].astype(f32)
+        self.state[1 - self.core] = whole_state(self.rc[...].astype(f32))
 
     def drain(self):
         self.swap().wait_send()
@@ -322,11 +361,12 @@
     (held_h, held_v, held_qk, weight_qk, flat, saved_w, saved_l, moved_q) = pop(8)
     (gs_h, gr_h, gs_v, gr_v, gs_q, gr_q) = pop(6)
     (ws, wr, us, ur, w_own, q_own) = pop(6)
-    (fs, fr, zcs, zcr, ss, sr) = pop(6)
+    (fs, fr, zcs, zcr, rys, ryr, ss, sr) = pop(8)
     early_bufs, late_bufs = pop(6), pop(6)
     early_sems, late_sems = pop(3), pop(3)
     (xin, cot, weights_t, weights_o) = pop(4)
-    (pp, cv, mix, gh, dn, phi_q, phi_k, states, grads, scaled, dconv) = pop(11)
+    (pp, cv, mix, gh, dn, phi_q, phi_k, states, grads, scaled) = pop(10)
+    dconv = pp
     (state_in, state_out, local_in, local_out, halo_in, halo_out) = pop(6)
     (first, second, moves) = pop(3)
     (x_sem, c_sem, w_sem, o_sem, r_sem, h_sem, k_sem) = pop(7)
@@ -334,9 +374,9 @@
     tp, place = lax.axis_index("tp"), lax.axis_index("seq")
 
     core, z = lax.rem(place, 2), lax.div(place, 2)
-    fwd = Ring("x", "y", [(held_h, CH, gs_h, gr_h)], *fwd_bufs, layer_out, fwd_sems)
+    fwd = Ring(1, [(held_h, CH, gs_h, gr_h)], *fwd_bufs, layer_out, fwd_sems)
     streams = [(held_v, CH, gs_v, gr_v), (held_qk, CH // 2, gs_q, gr_q)]
-    bwd = SplitRing("x", "y", streams, *bwd_bufs, input_grad, bwd_sems)
+    bwd = SplitRing(0, streams, *bwd_bufs, input_grad, bwd_sems)
     bwd.flat, bwd.weight_qk = flat, weight_qk
     early = Carry(True, local_in, state_in, early_bufs, early_sems)
     later = Carry(False, local_out, state_out, late_bufs, late_sems)
@@ -351,51 +391,50 @@
     def swap_device():
         return place + 1 - 2 * core
 
-    fwd_weights, fwd_swaps = [], []
-    for d in (1, 2, 3):
-        for j in range(2):
-            k = core * 2 + j
-            block = fwd.weight.at[k, d]
-            at = (d - 1, j)
-            fwd_weights.append(
-                to_device(
-                    out_block(block_at("x", d, "y", k)), block, ws.at[at], wr.at[at], neighbour("x", d)
+    sides = ((bwd.weight, 128, 0), (weight_qk, 32, 256))
+    fwd_weights, fwd_swaps, fwd_own, bwd_own = [], [], [], []
+    bwd_weights, spreads, relays, bwd_swaps = [], ([], []), ([], []), ([], [])
+    for p, (a, r) in enumerate((("x", "y"), ("y", "x"))):
+        for d in (1, 2, 3):
+            for j in range(2):
+                k = core * 2 + j
+                block = fwd.weight.at[p, k, d]
+                at = (p, d - 1, j)
+                wanted = out_block(block_at(a, d, r, k))
+                fwd_weights.append(to_device(wanted, block, ws.at[at], wr.at[at], neighbour(a, d)))
+                fwd_swaps.append(to_seq(block, block, us.at[at], ur.at[at], swap_device()))
+        for n, (array, size, start) in enumerate(sides):
+            half = rows_of(core, size)
+            theirs = pl.ds(pl.multiple_of(start + core * size, size), size)
+            for d in (1, 2, 3):
+                at = (p, n, d - 1)
+                wanted = weights_t.at[theirs, columns(block_at(a, d, r, z))]
+                bwd_weights.append(
+                    to_device(wanted, array.at[p, z, d, half], fs.at[at], fr.at[at], neighbour(a, d))
                 )
+            for n_way, step in enumerate((1, 3)):
+                at = (p, n, n_way)
+                there = lax.rem(z + step, 4) * 2 + core
+                mine = array.at[p, z, pl.ds(1, 3), half]
+                spreads[p].append(to_seq(mine, mine, zcs.at[at], zcr.at[at], there))
+                near = lax.rem(z + 4 - step, 4)
+                rows_in = pl.ds(
+                    pl.multiple_of(core * size + n_way * (size // 2), size // 2), size // 2
+                )
+                passing = array.at[p, near, pl.ds(1, 3), rows_in]
+                relays[p].append(to_seq(passing, passing, rys.at[at], ryr.at[at], there))
+            ours = array.at[p, :, pl.ds(1, 3), half]
+            bwd_swaps[p].append(to_seq(ours, ours, ss.at[p, n], sr.at[p, n], swap_device()))
+        for k in range(4):
+            t = block_at(a, 0, r, k)
+            fwd_own.append(
+                pltpu.make_async_copy(out_block(t), fwd.weight.at[p, k, 0], w_own.at[p, k])
             )
-            fwd_swaps.append(to_seq(block, block, us.at[at], ur.at[at], swap_device()))
-
-    sides = ((bwd.weight, 128, 0), (weight_qk, 32, 256))
-    bwd_weights, spreads, bwd_swaps = [], [], []
-    for n, (array, size, start) in enumerate(sides):
-        half = rows_of(core, size)
-        theirs = pl.ds(pl.multiple_of(start + core * size, size), size)
-        for d in (1, 2, 3):
-            at = (n, d - 1)
-            bwd_weights.append(
-                to_device(
-                    weights_t.at[theirs, columns(block_at("x", d, "y", z))],
-                    array.at[z, d, half],
-                    fs.at[at],
-                    fr.at[at],
-                    neighbour("x", d),
+            for n, (array, size, start) in enumerate(sides):
+                wanted = weights_t.at[pl.ds(start, 2 * size), columns(t)]
+                bwd_own.append(
+                    pltpu.make_async_copy(wanted, array.at[p, k, 0], q_own.at[p, n, k])
                 )
-            )
-            mine = array.at[z, pl.ds(1, 3), half]
-            there = lax.rem(z + d, 4) * 2 + core
-            spreads.append(to_seq(mine, mine, zcs.at[at], zcr.at[at], there))
-        ours = array.at[:, pl.ds(1, 3), half]
-        bwd_swaps.append(to_seq(ours, ours, ss.at[n], sr.at[n], swap_device()))
-
-    fwd_own, bwd_own = [], []
-    for k in range(4):
-        t = block_at("x", 0, "y", k)
-        fwd_own.append(pltpu.make_async_copy(out_block(t), fwd.weight.at[k, 0], w_own.at[0, k]))
-        for n, (array, size, start) in enumerate(sides):
-            bwd_own.append(
-                pltpu.make_async_copy(
-                    weights_t.at[pl.ds(start, 2 * size), columns(t)], array.at[k, 0], q_own.at[n, k]
-                )
-            )
 
     pieces = ((32, 128, 0), (192, 128, 128), (0, 32, 256), (160, 32, 288))
     w_loads = [
@@ -553,7 +592,7 @@
     early.late()
     for copy in bwd_weights:
         copy.wait()
-    for copy in spreads:
+    for copy in spreads[0]:
         copy.start()
     early.end()
     local_out[...] = jnp.zeros(local_out.shape, f32)
@@ -600,16 +639,20 @@
             d_qk = d_qk + dot((d_phi * a).astype(bf16), second[2 * h], NT)
         dconv[rows_of(c), 2 * DV : LANES] = d_qk
 
-        @pl.when(c == 1)
+        @pl.when(c == 0)
         def _():
             later.middle()
 
-        @pl.when(c == 3)
-        def _():
-            later.late()
-
-        fwd.forward(c)
-
+        @pl.when(c >= 1)
+        def _():
+            fwd.forward(c - 1)
+
+    fwd.forward(NCH - 1)
+    for copy in spreads[0]:
+        copy.wait()
+    for copy in relays[0]:
+        copy.start()
+    later.late()
     later.end()
     state_out[...] = state_out[...] + local_out[...]
 
@@ -643,6 +686,11 @@
         def _():
             behind.start()
 
+        @pl.when(c == 1)
+        def _():
+            for copy in spreads[1]:
+                copy.start()
+
         @pl.when(c > 0)
         def _():
             project_back(c - 1)
@@ -654,45 +702,64 @@
     behind.wait()
     dconv[pl.ds(NCH * CH, 8)] = halo_out[...] * one_if(place < 7)
     project_back(NCH - 1)
+
+    for copy in relays[0]:
+        copy.wait()
+    for copy in bwd_swaps[0]:
+        copy.start()
     for copy in fwd_swaps + fwd_own + bwd_own + res_loads:
         copy.wait()
 
-    @pl.loop(0, NCH + 3)
+    @pl.loop(0, NCH)
+    def _(j):
+        fwd.compute(j)
+
+    @pl.loop(0, 2)
+    def _(j):
+        bwd.forward(j)
+        bwd.send_own(j + 2)
+        fwd.send(j)
+
+    for copy in spreads[1]:
+        copy.wait()
+    for copy in relays[1]:
+        copy.start()
+    fwd.send(2)
+    fwd.send(3)
+    for copy in bwd_swaps[0]:
+        copy.wait()
+
+    @pl.loop(0, NCH + 1)
     def _(i):
-        @pl.when(i == 1)
-        def _():
-            for copy in spreads:
+        @pl.when(i < NCH)
+        def _():
+            bwd.multiply(i)
+
+        @pl.when(i == 0)
+        def _():
+            for copy in relays[1]:
                 copy.wait()
-            for copy in bwd_swaps:
+            for copy in bwd_swaps[1]:
                 copy.start()
 
-        @pl.when(i < NCH)
-        def _():
-            fwd.multiply(i)
-            bwd.forward(i)
-
-        @pl.when(i < NCH - 2)
-        def _():
-            bwd.send_own(i + 2)
-
-        @pl.when(i == 1)
-        def _():
-            for copy in bwd_swaps:
+        @pl.when(i < 2)
+        def _():
+            bwd.forward(i + 2)
+
+        @pl.when(i == 0)
+        def _():
+            for copy in bwd_swaps[1]:
                 copy.wait()
 
-        @pl.when((i >= 1) & (i < NCH + 1))
+        @pl.when(i >= 1)
         def _():
             fwd.relayed(i - 1)
-            bwd.multiply(i - 1)
-
-        @pl.when((i >= 2) & (i < NCH + 2))
-        def _():
-            bwd.relayed(i - 2)
-            fwd.finish(i - 2)
-
-        @pl.when(i >= 3)
-        def _():
-            bwd.finish(i - 3)
+            bwd.relayed(i - 1)
+
+    @pl.loop(0, NCH)
+    def _(i):
+        fwd.finish(i)
+        bwd.finish(i)
 
     @pl.loop(0, NCH)
     def _(c):
@@ -737,7 +804,8 @@
     result = jax.ShapeDtypeStruct((count, 256), bf16)
     dma = pltpu.SemaphoreType.DMA
     state = (DV, EXP)
-    carry_bufs = [pltpu.VMEM((n,) + state if n > 1 else state, bf16) for n in (1, 1, 1, 3, 1, 1)]
+    lump = (160, DV)
+    carry_bufs = [pltpu.VMEM((n,) + lump if n > 1 else lump, bf16) for n in (1, 1, 1, 3, 1, 1)]
     carry_sems = [dma((4,)), dma((3,)), dma((3,))]
     results = pl.pallas_call(
         layer_kernel,
@@ -752,17 +820,18 @@
             pltpu.VMEM((4, count, 256), bf16),
             pltpu.VMEM((4, count, 256), bf16),
             pltpu.VMEM((4, count // 2, 128), bf16),
-            pltpu.VMEM((4, 4, 64, 256), bf16),
+            pltpu.VMEM((2, 4, 4, 64, 256), bf16),
             pltpu.VMEM((CH, 256), bf16),
             pltpu.VMEM((HEADS, count, CH), bf16),
             pltpu.VMEM((HEADS, count, CH), f32),
             pltpu.VMEM((HEADS, count, 128), bf16),
         ]
         + [dma((3, NCH))] * 6
-        + [dma((3, 2))] * 4
-        + [dma((1, 4)), dma((2, 4))]
-        + [dma((2, 3))] * 4
-        + [dma((2,))] * 2
+        + [dma((2, 3, 2))] * 4
+        + [dma((2, 4)), dma((2, 2, 4))]
+        + [dma((2, 2, 3))] * 2
+        + [dma((2, 2, 2))] * 4
+        + [dma((2, 2))] * 2
         + carry_bufs
         + carry_bufs
         + carry_sems
@@ -782,7 +851,6 @@
             pltpu.VMEM((NCH, HEADS) + state, f32),
             pltpu.VMEM((NCH, HEADS) + state, f32),
             pltpu.VMEM((NCH, HEADS) + state, bf16),
-            pltpu.VMEM((count + 8, LANES), f32),
             pltpu.VMEM((HEADS,) + state, f32),
             pltpu.VMEM((HEADS,) + state, f32),
             pltpu.VMEM((HEADS,) + state, f32),
@@ -801,7 +869,7 @@
             dma((3,)),
         ],
         compiler_params=pltpu.CompilerParams(
-            collective_id=0, has_side_effects=True, vmem_limit_bytes=62 << 20
+            collective_id=0, has_side_effects=True, vmem_limit_bytes=67043328
         ),
     )(
         inputs,

time: 92.6 us -> 79.3 us (0.86)
  Pallas kernels: 91.8 us -> 77.8 us
    pallas_call x1, Pallas kernels: 89.8 us -> 75.8 us  [per_device(): pl.pallas_call(layer_kernel, out_shape=(result, result), in_specs=[whole]...]
where the time goes in v3:
time: 79.3 us; the launch traced here: 78.5 us
  Pallas kernels  77.8 us (98%)
    pallas_call x1, Pallas kernels, per_device(): pl.pallas_call(layer_kernel, out_shape=(result, result), in_specs=[whole]...  75.8 us
    pallas_call x1, Pallas kernels, settle(): pl.pallas_call(settle_kernel, out_shape=(result, result), in_specs=[whole...  2.04 us

profile of v3, /device:TPU:1, one launch (start us, length us, event | category | flops | bytes accessed | tf_op | source)
XLA Modules:
  0.0 78.5 jit_solution(7591064260907014120)
XLA Ops:
  0.6 75.8 %shard_map.122 = (bf16[1024,256]{1,0:T(8,128)(2,1)}, bf16[1024,256]{1,0:T(8,128)(2,1)}) custom-call(bf16[1024,4096]{1,0:T(8,128)(2,1)} %inputs.1, bf16[1024,4096]{1,0:T(8,128)(2,1)} %cotangent.1, bf16[320,4096]{1,0:T(8,128)(2,1)} %bitcast.2, bf16[256,4096]{1,0:T(8,128)(2,1)} %w_out.1, bf16[4,128,256]{2,1,0:T(8,128)(2,1)} %constant.8.clone.first_any, ...), custom_call_target="tpu_custom_call" | custom-call | tf_op jit(solution)/shard_map/pallas_call | solution.py:810
  76.4 2.0 %shard_map.123 = (bf16[1024,256]{1,0:T(8,128)(2,1)}, bf16[1024,256]{1,0:T(8,128)(2,1)}) custom-call(bf16[1024,256]{1,0:T(8,128)(2,1)} %get-tuple-element.4.first, bf16[1024,256]{1,0:T(8,128)(2,1)} %get-tuple-element.5.second), custom_call_target="tpu_custom_call" | custom-call | tf_op jit(solution)/shard_map/pallas_call | solution.py:790

commit v4 on v3

--- a/solution.py
+++ b/solution.py
@@ -604,7 +604,7 @@
             state_in[h] = entering + states[c, h]
             scaled[c, h] = (entering * scale).astype(bf16)
             numerator = mix[rows_of(c), lanes(h)] + dot(phi_q[h, rows_of(c)], scaled[c, h], NT)
-            inverse = 1.0 / jnp.sqrt(jnp.mean(numerator * numerator, -1, keepdims=True) + epsilon)
+            inverse = lax.rsqrt(jnp.mean(numerator * numerator, -1, keepdims=True) + epsilon)
             normed = numerator * inverse
             heads[rows_of(c), lanes(h)] = (normed * gain[:, lanes(h)]).astype(bf16)
             grad = gh[rows_of(c), lanes(h)]
@@ -695,18 +695,15 @@
         def _():
             project_back(c - 1)
 
-        @pl.when((c == 1) | (c == 2))
+        @pl.when(c > 0)
         def _():
             bwd.send_own(c - 1)
 
     behind.wait()
     dconv[pl.ds(NCH * CH, 8)] = halo_out[...] * one_if(place < 7)
     project_back(NCH - 1)
-
-    for copy in relays[0]:
-        copy.wait()
-    for copy in bwd_swaps[0]:
-        copy.start()
+    bwd.send_own(NCH - 1)
+
     for copy in fwd_swaps + fwd_own + bwd_own + res_loads:
         copy.wait()
 
@@ -714,22 +711,24 @@
     def _(j):
         fwd.compute(j)
 
-    @pl.loop(0, 2)
+    @pl.loop(0, NCH)
     def _(j):
         bwd.forward(j)
-        bwd.send_own(j + 2)
         fwd.send(j)
 
-    for copy in spreads[1]:
+        @pl.when(j == 1)
+        def _():
+            for copy in relays[0] + spreads[1]:
+                copy.wait()
+            for copy in bwd_swaps[0] + relays[1]:
+                copy.start()
+
+    for copy in bwd_swaps[0] + relays[1]:
         copy.wait()
-    for copy in relays[1]:
+    for copy in bwd_swaps[1]:
         copy.start()
-    fwd.send(2)
-    fwd.send(3)
-    for copy in bwd_swaps[0]:
-        copy.wait()
-
-    @pl.loop(0, NCH + 1)
+
+    @pl.loop(0, NCH + 3)
     def _(i):
         @pl.when(i < NCH)
         def _():
@@ -737,24 +736,16 @@
 
         @pl.when(i == 0)
         def _():
-            for copy in relays[1]:
-                copy.wait()
-            for copy in bwd_swaps[1]:
-                copy.start()
-
-        @pl.when(i < 2)
-        def _():
-            bwd.forward(i + 2)
-
-        @pl.when(i == 0)
-        def _():
             for copy in bwd_swaps[1]:
                 copy.wait()
 
-        @pl.when(i >= 1)
+        @pl.when((i >= 1) & (i < NCH + 1))
         def _():
             fwd.relayed(i - 1)
-            bwd.relayed(i - 1)
+
+        @pl.when(i >= 3)
+        def _():
+            bwd.relayed(i - 3)
 
     @pl.loop(0, NCH)
     def _(i):

time: 79.3 us -> 74.7 us (0.942)
  Pallas kernels: 77.8 us -> 73.8 us
    pallas_call x1, Pallas kernels: 75.8 us -> 71.8 us  [per_device(): pl.pallas_call(layer_kernel, out_shape=(result, result), in_specs=[whole]...]
where the time goes in v4:
time: 74.7 us; the launch traced here: 74.5 us
  Pallas kernels  73.8 us (99%)
    pallas_call x1, Pallas kernels, per_device(): pl.pallas_call(layer_kernel, out_shape=(result, result), in_specs=[whole]...  71.8 us
    pallas_call x1, Pallas kernels, settle(): pl.pallas_call(settle_kernel, out_shape=(result, result), in_specs=[whole...  2.04 us

profile of v4, /device:TPU:1, one launch (start us, length us, event | category | flops | bytes accessed | tf_op | source)
XLA Modules:
  0.0 74.5 jit_solution(11598089286154819736)
XLA Ops:
  0.6 71.8 %shard_map.122 = (bf16[1024,256]{1,0:T(8,128)(2,1)}, bf16[1024,256]{1,0:T(8,128)(2,1)}) custom-call(bf16[1024,4096]{1,0:T(8,128)(2,1)} %inputs.1, bf16[1024,4096]{1,0:T(8,128)(2,1)} %cotangent.1, bf16[320,4096]{1,0:T(8,128)(2,1)} %bitcast.2, bf16[256,4096]{1,0:T(8,128)(2,1)} %w_out.1, bf16[4,128,256]{2,1,0:T(8,128)(2,1)} %constant.8.clone.first_any, ...), custom_call_target="tpu_custom_call" | custom-call | tf_op jit(solution)/shard_map/pallas_call | solution.py:801
  72.4 2.0 %shard_map.123 = (bf16[1024,256]{1,0:T(8,128)(2,1)}, bf16[1024,256]{1,0:T(8,128)(2,1)}) custom-call(bf16[1024,256]{1,0:T(8,128)(2,1)} %get-tuple-element.4.first, bf16[1024,256]{1,0:T(8,128)(2,1)} %get-tuple-element.5.second), custom_call_target="tpu_custom_call" | custom-call | tf_op jit(solution)/shard_map/pallas_call | solution.py:781

commit v5 on v4

--- a/solution.py
+++ b/solution.py
@@ -80,7 +80,7 @@
         self.flip, self.streams, self.weight = flip, streams, weight
         self.part, self.landed, self.relay = part, landed, relay
         self.keep, self.res, self.out = keep, res, out
-        (self.ts, self.tr, self.ps, self.pr, self.os) = sems
+        (self.ps, self.tr, self.pr, self.os) = sems
 
     def turn(self, c):
         return lax.rem(c + self.flip, 2)
@@ -96,7 +96,7 @@
             to_device(
                 held.at[0, rows_of(c, size)],
                 held.at[d, rows_of(c, size)],
-                send.at[d - 1, c],
+                send.at[0],
                 recv.at[d - 1, c],
                 self.gather_to(c, d),
             )
@@ -108,7 +108,7 @@
             to_device(
                 held.at[way(c), rows_of(c, size)],
                 held.at[2, rows_of(c, size)],
-                send.at[1, c],
+                send.at[0],
                 recv.at[1, c],
                 self.gather_to(c, way(c)),
             )
@@ -131,7 +131,7 @@
         return to_device(
             self.part.at[2, rows_of(c)],
             self.relay.at[rows_of(c)],
-            self.ts.at[c],
+            self.ps.at[0],
             self.tr.at[c],
             self.scatter_to(c, way(c)),
         )
@@ -140,7 +140,7 @@
         return to_device(
             self.part.at[d, rows_of(c)],
             self.landed.at[d // 2, rows_of(c)],
-            self.ps.at[d // 2, c],
+            self.ps.at[0],
             self.pr.at[d // 2, c],
             self.scatter_to(c, d),
         )
@@ -200,16 +200,16 @@
 
     def leave(self, c):
         return pltpu.make_async_copy(
-            self.part.at[0, rows_of(c)], self.out.at[rows_of(c)], self.os.at[c]
+            self.part.at[0, rows_of(c)], self.out.at[rows_of(c)], self.os.at[0]
         )
 
-    def drain(self, c):
-        for copy in self.direct(c, 1) + self.direct(c, 3) + self.passed_on(c):
-            copy.wait_send()
-        self.tie(c).wait_send()
-        self.side(c, 1).wait_send()
-        self.side(c, 3).wait_send()
-        self.leave(c).wait()
+    def drain(self):
+        for held, _, send, recv in self.streams:
+            sent = held.at[pl.ds(1, 3)]
+            to_device(sent, sent, send.at[0], recv.at[0, 0], self.gather_to(0, 1)).wait_send()
+        sent = self.part.at[pl.ds(1, 3)]
+        to_device(sent, sent, self.ps.at[0], self.tr.at[0], self.scatter_to(0, 1)).wait_send()
+        pltpu.make_async_copy(self.part.at[0], self.out, self.os.at[0]).wait()
 
 
 class SplitRing(Ring):
@@ -231,7 +231,7 @@
 
 def ring_semaphores():
     dma = pltpu.SemaphoreType.DMA
-    return [dma((NCH,)), dma((NCH,)), dma((2, NCH)), dma((2, NCH)), dma((NCH,))]
+    return [dma((1,)), dma((NCH,)), dma((2, NCH)), dma((1,))]
 
 
 def ring_buffers(rows):
@@ -357,7 +357,7 @@
         return got
 
     fwd_bufs, bwd_bufs = pop(6), pop(6)
-    fwd_sems, bwd_sems = pop(5), pop(5)
+    fwd_sems, bwd_sems = pop(4), pop(4)
     (held_h, held_v, held_qk, weight_qk, flat, saved_w, saved_l, moved_q) = pop(8)
     (gs_h, gr_h, gs_v, gr_v, gs_q, gr_q) = pop(6)
     (ws, wr, us, ur, w_own, q_own) = pop(6)
@@ -399,21 +399,18 @@
             for j in range(2):
                 k = core * 2 + j
                 block = fwd.weight.at[p, k, d]
-                at = (p, d - 1, j)
                 wanted = out_block(block_at(a, d, r, k))
-                fwd_weights.append(to_device(wanted, block, ws.at[at], wr.at[at], neighbour(a, d)))
-                fwd_swaps.append(to_seq(block, block, us.at[at], ur.at[at], swap_device()))
+                fwd_weights.append(to_device(wanted, block, ws.at[0], wr.at[0], neighbour(a, d)))
         for n, (array, size, start) in enumerate(sides):
             half = rows_of(core, size)
             theirs = pl.ds(pl.multiple_of(start + core * size, size), size)
             for d in (1, 2, 3):
-                at = (p, n, d - 1)
                 wanted = weights_t.at[theirs, columns(block_at(a, d, r, z))]
                 bwd_weights.append(
-                    to_device(wanted, array.at[p, z, d, half], fs.at[at], fr.at[at], neighbour(a, d))
+                    to_device(wanted, array.at[p, z, d, half], fs.at[n], fr.at[n], neighbour(a, d))
                 )
             for n_way, step in enumerate((1, 3)):
-                at = (p, n, n_way)
+                at = (p, n)
                 there = lax.rem(z + step, 4) * 2 + core
                 mine = array.at[p, z, pl.ds(1, 3), half]
                 spreads[p].append(to_seq(mine, mine, zcs.at[at], zcr.at[at], there))
@@ -428,13 +425,31 @@
         for k in range(4):
             t = block_at(a, 0, r, k)
             fwd_own.append(
-                pltpu.make_async_copy(out_block(t), fwd.weight.at[p, k, 0], w_own.at[p, k])
+                pltpu.make_async_copy(out_block(t), fwd.weight.at[p, k, 0], w_own.at[0])
             )
             for n, (array, size, start) in enumerate(sides):
                 wanted = weights_t.at[pl.ds(start, 2 * size), columns(t)]
                 bwd_own.append(
-                    pltpu.make_async_copy(wanted, array.at[p, k, 0], q_own.at[p, n, k])
+                    pltpu.make_async_copy(wanted, array.at[p, k, 0], q_own.at[n])
                 )
+
+    fetched = fwd.weight.at[:, pl.ds(core * 2, 2), pl.ds(1, 3)]
+    fwd_fetch = to_device(fetched, fetched, ws.at[0], wr.at[0], neighbour("x", 1))
+    fwd_swaps.append(to_seq(fetched, fetched, us.at[0], ur.at[0], swap_device()))
+    owned = fwd.weight.at[:, :, 0]
+    own_waits = [pltpu.make_async_copy(owned, owned, w_own.at[0])]
+    bwd_fetch, spread_waits, relay_waits = [], ([], []), ([], [])
+    for n, (array, size, start) in enumerate(sides):
+        owned = array.at[:, :, 0]
+        own_waits.append(pltpu.make_async_copy(owned, owned, q_own.at[n]))
+        fetched = array.at[:, z, pl.ds(1, 3), rows_of(core, size)]
+        bwd_fetch.append(to_device(fetched, fetched, fs.at[n], fr.at[n], neighbour("x", 1)))
+        for p in range(2):
+            both = array.at[p, pl.ds(0, 2), pl.ds(1, 3), rows_of(core, size)]
+            one = array.at[p, z, pl.ds(1, 3), rows_of(core, size)]
+            there = lax.rem(z + 1, 4) * 2 + core
+            spread_waits[p].append(to_seq(both, both, zcs.at[p, n], zcr.at[p, n], there))
+            relay_waits[p].append(to_seq(one, one, rys.at[p, n], ryr.at[p, n], there))
 
     pieces = ((32, 128, 0), (192, 128, 128), (0, 32, 256), (160, 32, 288))
     w_loads = [
@@ -590,7 +605,7 @@
             phi_q[h, rows_of(c)] = (a * b).astype(bf16)
 
     early.late()
-    for copy in bwd_weights:
+    for copy in bwd_fetch:
         copy.wait()
     for copy in spreads[0]:
         copy.start()
@@ -617,8 +632,7 @@
         fwd.send_own(c)
 
     later.start()
-    for copy in fwd_weights:
-        copy.wait()
+    fwd_fetch.wait()
     for copy in fwd_swaps:
         copy.start()
 
@@ -648,7 +662,7 @@
             fwd.forward(c - 1)
 
     fwd.forward(NCH - 1)
-    for copy in spreads[0]:
+    for copy in spread_waits[0]:
         copy.wait()
     for copy in relays[0]:
         copy.start()
@@ -704,7 +718,7 @@
     project_back(NCH - 1)
     bwd.send_own(NCH - 1)
 
-    for copy in fwd_swaps + fwd_own + bwd_own + res_loads:
+    for copy in fwd_swaps + own_waits + res_loads:
         copy.wait()
 
     @pl.loop(0, NCH)
@@ -718,15 +732,13 @@
 
         @pl.when(j == 1)
         def _():
-            for copy in relays[0] + spreads[1]:
+            for copy in relay_waits[0] + spread_waits[1]:
                 copy.wait()
             for copy in bwd_swaps[0] + relays[1]:
                 copy.start()
 
-    for copy in bwd_swaps[0] + relays[1]:
+    for copy in bwd_swaps[0]:
         copy.wait()
-    for copy in bwd_swaps[1]:
-        copy.start()
 
     @pl.loop(0, NCH + 3)
     def _(i):
@@ -736,6 +748,10 @@
 
         @pl.when(i == 0)
         def _():
+            for copy in relay_waits[1]:
+                copy.wait()
+            for copy in bwd_swaps[1]:
+                copy.start()
             for copy in bwd_swaps[1]:
                 copy.wait()
 
@@ -752,10 +768,8 @@
         fwd.finish(i)
         bwd.finish(i)
 
-    @pl.loop(0, NCH)
-    def _(c):
-        fwd.drain(c)
-        bwd.drain(c)
+    fwd.drain()
+    bwd.drain()
 
     early.drain()
     later.drain()
@@ -817,11 +831,11 @@
             pltpu.VMEM((HEADS, count, CH), f32),
             pltpu.VMEM((HEADS, count, 128), bf16),
         ]
-        + [dma((3, NCH))] * 6
-        + [dma((2, 3, 2))] * 4
-        + [dma((2, 4)), dma((2, 2, 4))]
-        + [dma((2, 2, 3))] * 2
-        + [dma((2, 2, 2))] * 4
+        + [dma((1,)), dma((3, NCH))] * 3
+        + [dma((1,))] * 4
+        + [dma((1,)), dma((2,))]
+        + [dma((2,))] * 2
+        + [dma((2, 2))] * 4
         + [dma((2, 2))] * 2
         + carry_bufs
         + carry_bufs

time: 74.7 us -> 73.8 us (0.988)
  Pallas kernels: 73.8 us -> 73 us
    pallas_call x1, Pallas kernels: 71.8 us -> 70.9 us  [per_device(): pl.pallas_call(layer_kernel, out_shape=(result, result), in_specs=[whole]...]
where the time goes in v5:
time: 73.8 us; the launch traced here: 73.6 us
  Pallas kernels  73 us (99%)
    pallas_call x1, Pallas kernels, per_device(): pl.pallas_call(layer_kernel, out_shape=(result, result), in_specs=[whole]...  70.9 us
    pallas_call x1, Pallas kernels, settle(): pl.pallas_call(settle_kernel, out_shape=(result, result), in_specs=[whole...  2.04 us

profile of v5, /device:TPU:1, one launch (start us, length us, event | category | flops | bytes accessed | tf_op | source)
XLA Modules:
  0.0 73.6 jit_solution(4810445176422604092)
XLA Ops:
  0.6 70.9 %shard_map.122 = (bf16[1024,256]{1,0:T(8,128)(2,1)}, bf16[1024,256]{1,0:T(8,128)(2,1)}) custom-call(bf16[1024,4096]{1,0:T(8,128)(2,1)} %inputs.1, bf16[1024,4096]{1,0:T(8,128)(2,1)} %cotangent.1, bf16[320,4096]{1,0:T(8,128)(2,1)} %bitcast.2, bf16[256,4096]{1,0:T(8,128)(2,1)} %w_out.1, bf16[4,128,256]{2,1,0:T(8,128)(2,1)} %constant.8.clone.first_any, ...), custom_call_target="tpu_custom_call" | custom-call | tf_op jit(solution)/shard_map/pallas_call | solution.py:815
  71.6 2.0 %shard_map.123 = (bf16[1024,256]{1,0:T(8,128)(2,1)}, bf16[1024,256]{1,0:T(8,128)(2,1)}) custom-call(bf16[1024,256]{1,0:T(8,128)(2,1)} %get-tuple-element.4.first, bf16[1024,256]{1,0:T(8,128)(2,1)} %get-tuple-element.5.second), custom_call_target="tpu_custom_call" | custom-call | tf_op jit(solution)/shard_map/pallas_call | solution.py:795

commit v6 on v5

--- a/solution.py
+++ b/solution.py
@@ -699,9 +699,6 @@
         @pl.when(c == 0)
         def _():
             behind.start()
-
-        @pl.when(c == 1)
-        def _():
             for copy in spreads[1]:
                 copy.start()
 
@@ -730,7 +727,7 @@
         bwd.forward(j)
         fwd.send(j)
 
-        @pl.when(j == 1)
+        @pl.when(j == 0)
         def _():
             for copy in relay_waits[0] + spread_waits[1]:
                 copy.wait()

time: 73.8 us -> 73.8 us (level)
  no operation moved by 1% of the time
where the time goes in v6:
time: 73.8 us; the launch traced here: 73.6 us
  Pallas kernels  73 us (99%)
    pallas_call x1, Pallas kernels, per_device(): pl.pallas_call(layer_kernel, out_shape=(result, result), in_specs=[whole]...  70.9 us
    pallas_call x1, Pallas kernels, settle(): pl.pallas_call(settle_kernel, out_shape=(result, result), in_specs=[whole...  2.04 us

profile of v6, /device:TPU:1, one launch (start us, length us, event | category | flops | bytes accessed | tf_op | source)
XLA Modules:
  0.0 73.6 jit_solution(1777100940526349705)
XLA Ops:
  0.6 70.9 %shard_map.122 = (bf16[1024,256]{1,0:T(8,128)(2,1)}, bf16[1024,256]{1,0:T(8,128)(2,1)}) custom-call(bf16[1024,4096]{1,0:T(8,128)(2,1)} %inputs.1, bf16[1024,4096]{1,0:T(8,128)(2,1)} %cotangent.1, bf16[320,4096]{1,0:T(8,128)(2,1)} %bitcast.2, bf16[256,4096]{1,0:T(8,128)(2,1)} %w_out.1, bf16[4,128,256]{2,1,0:T(8,128)(2,1)} %constant.8.clone.first_any, ...), custom_call_target="tpu_custom_call" | custom-call | tf_op jit(solution)/shard_map/pallas_call | solution.py:812
  71.6 2.0 %shard_map.123 = (bf16[1024,256]{1,0:T(8,128)(2,1)}, bf16[1024,256]{1,0:T(8,128)(2,1)}) custom-call(bf16[1024,256]{1,0:T(8,128)(2,1)} %get-tuple-element.4.first, bf16[1024,256]{1,0:T(8,128)(2,1)} %get-tuple-element.5.second), custom_call_target="tpu_custom_call" | custom-call | tf_op jit(solution)/shard_map/pallas_call | solution.py:792

commit v7 on v6

--- a/solution.py
+++ b/solution.py
@@ -739,6 +739,10 @@
 
     @pl.loop(0, NCH + 3)
     def _(i):
+        @pl.when((i >= 1) & (i < NCH + 1))
+        def _():
+            fwd.relayed(i - 1)
+
         @pl.when(i < NCH)
         def _():
             bwd.multiply(i)
@@ -751,10 +755,6 @@
                 copy.start()
             for copy in bwd_swaps[1]:
                 copy.wait()
-
-        @pl.when((i >= 1) & (i < NCH + 1))
-        def _():
-            fwd.relayed(i - 1)
 
         @pl.when(i >= 3)
         def _():

time: 73.8 us -> 73.3 us (level)
  no operation moved by 1% of the time
where the time goes in v7:
time: 73.3 us; the launch traced here: 73 us
  Pallas kernels  72.3 us (99%)
    pallas_call x1, Pallas kernels, per_device(): pl.pallas_call(layer_kernel, out_shape=(result, result), in_specs=[whole]...  70.3 us
    pallas_call x1, Pallas kernels, settle(): pl.pallas_call(settle_kernel, out_shape=(result, result), in_specs=[whole...  2.04 us

profile of v7, /device:TPU:1, one launch (start us, length us, event | category | flops | bytes accessed | tf_op | source)
XLA Modules:
  0.0 73.0 jit_solution(10522286802244517965)
XLA Ops:
  0.6 70.3 %shard_map.122 = (bf16[1024,256]{1,0:T(8,128)(2,1)}, bf16[1024,256]{1,0:T(8,128)(2,1)}) custom-call(bf16[1024,4096]{1,0:T(8,128)(2,1)} %inputs.1, bf16[1024,4096]{1,0:T(8,128)(2,1)} %cotangent.1, bf16[320,4096]{1,0:T(8,128)(2,1)} %bitcast.2, bf16[256,4096]{1,0:T(8,128)(2,1)} %w_out.1, bf16[4,128,256]{2,1,0:T(8,128)(2,1)} %constant.8.clone.first_any, ...), custom_call_target="tpu_custom_call" | custom-call | tf_op jit(solution)/shard_map/pallas_call | solution.py:812
  70.9 2.0 %shard_map.123 = (bf16[1024,256]{1,0:T(8,128)(2,1)}, bf16[1024,256]{1,0:T(8,128)(2,1)}) custom-call(bf16[1024,256]{1,0:T(8,128)(2,1)} %get-tuple-element.4.first, bf16[1024,256]{1,0:T(8,128)(2,1)} %get-tuple-element.5.second), custom_call_target="tpu_custom_call" | custom-call | tf_op jit(solution)/shard_map/pallas_call | solution.py:792
